TPU v7x, 32 devices: a whole 2x2x4 slice. The times are simulated.
32 devices in a mesh: cell: 4 (over y, x), chan: 8 (over z, core).
Axes of the slice: x: 2, y: 2, z: 4, core: 2. Of those that a mesh axis runs over, the one named last changes fastest.
Arguments:
- slab: bfloat16 [32768, 8192], P('cell', 'chan'), may hold values from -6 to 6
- cell_factor: float32 [32, 32768], P(None, 'cell'), may hold values from -6 to 6
- chan_factor: float32 [32, 8192], P(None, 'chan'), may hold values from -6 to 6
- cell_mttkrp: float32 [32, 32768], P(None, 'cell'), may hold values from -12 to 12
- chan_mttkrp: float32 [32, 8192], P(None, 'chan'), may hold values from -12 to 12
- cell_gram_acc: float32 [32, 32], replicated, as said below
- chan_gram_acc: float32 [32, 32], replicated, as said below
Outputs:
- time_row: float32 [32], replicated
- new_cell_factor: float32 [32, 32768], P(None, 'cell')
- new_chan_factor: float32 [32, 8192], P(None, 'chan')
- new_cell_mttkrp: float32 [32, 32768], P(None, 'cell')
- new_chan_mttkrp: float32 [32, 8192], P(None, 'chan')
- new_cell_gram: float32 [32, 32], replicated
- new_chan_gram: float32 [32, 32], replicated
Inputs may be any that keep to these rules, and one draw needn't show every extreme that they name: `cell_gram_acc`: symmetric with a dominant positive diagonal. `chan_gram_acc`: symmetric with a dominant positive diagonal.
All inputs are finite; a program needn't handle non-finite values.
Results may differ from a plain program's by a relative error of at most 0.0033.
Values sent between devices are 32-bit elements; how exact they have to be, the bound alone decides.
No kernel may reach another device: no remote copies, remote signals or barrier semaphores. Data moves between devices by JAX's collectives and lax.ppermute only.
A program may use at most 64 MiB of HBM per device.

v0:
```python
import math

import jax
import jax.numpy as jnp
from jax import lax
from jax.sharding import PartitionSpec as P


def spd_solve(matrix, right):
    lower = jnp.linalg.cholesky(matrix)
    return jax.scipy.linalg.cho_solve((lower, True), right)


def body(slab, cell_factor, chan_factor, cell_mttkrp, chan_mttkrp, cell_gram_acc, chan_gram_acc):
    hi = lax.Precision.HIGHEST
    n_cell = lax.axis_size("cell")
    n_chan = lax.axis_size("chan")
    local_rows = slab.shape[0]
    local_cols = slab.shape[1]
    all_rows = local_rows * n_cell
    all_cols = local_cols * n_chan
    chan_low = chan_factor.astype(jnp.bfloat16)
    slab_chan = lax.dot_general(
        chan_low, slab, (((1,), (1,)), ((), ())), preferred_element_type=jnp.float32
    )
    rhs_part = jnp.sum(cell_factor * slab_chan, axis=1) / math.sqrt(all_rows * all_cols)
    cell_part = jnp.dot(cell_factor, cell_factor.T, precision=hi) / all_rows
    chan_part = jnp.dot(chan_factor, chan_factor.T, precision=hi) / all_cols
    rhs = lax.psum(rhs_part, ("cell", "chan"))
    cell_norm = lax.psum(cell_part, "cell")
    chan_norm = lax.psum(chan_part, "chan")
    time_row = spd_solve(cell_norm * chan_norm, rhs[:, None])[:, 0]
    outer = time_row[:, None] * time_row[None, :]
    new_cell_gram = cell_gram_acc + chan_norm * outer
    summed = lax.psum(slab_chan, "chan")
    new_cell_mttkrp = cell_mttkrp + time_row[:, None] * summed / math.sqrt(all_cols)
    new_cell_factor = spd_solve(new_cell_gram, new_cell_mttkrp)
    local_gram = jnp.dot(new_cell_factor, new_cell_factor.T, precision=hi) / all_rows
    new_norm = lax.psum(local_gram, "cell")
    cell_low = new_cell_factor.astype(jnp.bfloat16)
    slab_cell = jnp.dot(cell_low, slab, preferred_element_type=jnp.float32)
    cell_summed = lax.psum(slab_cell, "cell")
    new_chan_mttkrp = chan_mttkrp + time_row[:, None] * cell_summed / math.sqrt(all_rows)
    new_chan_gram = chan_gram_acc + new_norm * outer
    new_chan_factor = spd_solve(new_chan_gram, new_chan_mttkrp)
    return (
        time_row,
        new_cell_factor,
        new_chan_factor,
        new_cell_mttkrp,
        new_chan_mttkrp,
        new_cell_gram,
        new_chan_gram,
    )


def solution(mesh):
    placed = (
        P("cell", "chan"),
        P(None, "cell"),
        P(None, "chan"),
        P(None, "cell"),
        P(None, "chan"),
        P(),
        P(),
    )
    return jax.shard_map(
        body,
        mesh=mesh,
        in_specs=placed,
        out_specs=(
            P(),
            P(None, "cell"),
            P(None, "chan"),
            P(None, "cell"),
            P(None, "chan"),
            P(),
            P(),
        ),
        check_vma=False,
    )
```

profile of v0, /device:TPU:0, one launch (start us, length us, event | category | flops | bytes accessed | tf_op | source)
XLA Modules:
  0.0 202.9 jit_solution(13627783786792271417)
XLA Ops:
  7.2 0.0 copy-start.3
  7.2 0.0 copy-start.1
  7.2 0.0 copy-start.10
  7.2 0.0 copy-start.11
  7.2 0.0 copy-start.4
  7.2 0.0 all-reduce.3.cloned.1.call-start
  7.3 12.4 %multiply_reduce_fusion = (f32[32]{0:T(128)S(1)}, f32[32,8192]{1,0:T(8,128)}) fusion(f32[32,8192]{1,0:T(8,128)} %param.9, bf16[8192,1024]{1,0:T(8,128)(2,1)} %param.8, f32[32,1024]{1,0:T(8,128)} %param.10), kind=kOutput, calls=%fused_computation.6 | convolution fusion | flops 537427968 | bytes 19005568 | tf_op jit(solution)/shard_map/dot_general | solution.py:23
  19.6 0.0 all-reduce.3.cloned.1.call-update
  19.7 0.0 all-reduce.5.cloned.1.call-start
  19.7 0.0 copy-done.3
  19.7 0.2 convolution_multiply_fusion.1
  20.0 0.0 copy-done.1
  20.0 1.0 convolution_multiply_fusion.2
  21.0 30.4 %psum.43 = f32[32,32]{0,1:T(8,128)S(1)} all-reduce(f32[32,32]{0,1:T(8,128)S(1)} %convolution_multiply_fusion.1), channel_id=1, replica_groups=mesh['cell'=4,'chan'=8] {'chan'}, use_global_device_ids=true, to_apply=%region_1.0 | all-reduce | flops 1024 | bytes 8192 | tf_op jit(solution)/shard_map/psum | solution.py:31
  51.3 16.0 %psum.42 = f32[32,32]{0,1:T(8,128)S(1)} all-reduce(f32[32,32]{0,1:T(8,128)S(1)} %convolution_multiply_fusion.2), channel_id=1, replica_groups=mesh['cell'=4,'chan'=8] {'cell'}, use_global_device_ids=true, to_apply=%region_0.0 | all-reduce | flops 1024 | bytes 8192 | tf_op jit(solution)/shard_map/psum | solution.py:30
  67.4 0.1 copy.16
  67.4 2.9 %cholesky.59 = f32[32,32]{1,0:T(8,128)S(1)} custom-call(f32[32,32]{1,0:T(8,128)S(1)} %fusion.21), custom_call_target="Cholesky" | custom-call | tf_op jit(solution)/shard_map/jit(cholesky)/cholesky | solution.py:10
  70.4 0.6 compare_reduce_fusion.2
  71.0 0.7 fusion.4
  71.7 2.4 %custom-call.23 = f32[1,32,32]{1,2,0:T(8,128)S(1)} custom-call(f32[1,32,32]{2,1,0:T(8,128)S(1)} %fusion.4), custom_call_target="InvertDiagBlocksLowerTriangular" | custom-call | tf_op jit(solution)/shard_map/jit(_cho_solve)/triangular_solve | solution.py:11
  74.1 37.0 %psum.44 = f32[32]{0:T(128)S(1)} all-reduce(f32[32]{0:T(128)S(1)} %broadcast_multiply_fusion), channel_id=1, replica_groups=mesh['cell'=4,'chan'=8] {'cell','chan'}, use_global_device_ids=true, to_apply=%region_5.7 | all-reduce | flops 32 | bytes 256 | tf_op jit(solution)/shard_map/psum | solution.py:29
  111.2 0.1 convolution_bitcast_fusion.1
  111.3 0.1 convolution_bitcast_fusion
  111.4 0.0 copy-done.10
  111.5 0.1 copy.17
  111.5 0.1 fusion.7
  111.6 0.1 copy.18
  111.7 0.0 copy-start.7
  111.7 2.9 %cholesky.70 = f32[32,32]{1,0:T(8,128)S(1)} custom-call(f32[32,32]{1,0:T(8,128)S(1)} %fusion.18), custom_call_target="Cholesky" | custom-call | tf_op jit(solution)/shard_map/jit(cholesky)/cholesky | solution.py:10
  114.7 0.6 compare_reduce_fusion.1
  115.3 0.7 fusion.5
  116.0 2.4 %custom-call.24 = f32[1,32,32]{1,2,0:T(8,128)S(1)} custom-call(f32[1,32,32]{2,1,0:T(8,128)S(1)} %fusion.5), custom_call_target="InvertDiagBlocksLowerTriangular" | custom-call | tf_op jit(solution)/shard_map/jit(_cho_solve)/triangular_solve | solution.py:11
  118.4 0.0 copy-done.11
  118.4 0.1 copy.20
  118.5 0.0 all-reduce.3.cloned.1.call-done
  118.5 0.0 copy-done.4
  118.5 1.4 multiply_add_fusion
  119.9 0.0 copy-start.2
  119.9 0.0 copy-start.6
  119.9 1.0 fusion.16
  121.0 1.0 fusion.14
  122.0 0.0 copy-start
  122.0 1.0 convolution_multiply_fusion
  123.0 9.4 %fusion = f32[32,1024]{1,0:T(8,128)} fusion(bf16[8192,1024]{1,0:T(8,128)(2,1)} %param.8, f32[32,8192]{1,0:T(8,128)S(1)} %fusion.14), kind=kOutput, calls=%fused_computation.7 | convolution fusion | flops 537133056 | bytes 17956864 | tf_op jit(solution)/shard_map/dot_general | solution.py:41
  132.4 0.0 copy-done.7
  132.4 15.9 %psum.46 = f32[32,32]{0,1:T(8,128)S(1)} all-reduce(f32[32,32]{0,1:T(8,128)S(1)} %convolution_multiply_fusion), channel_id=1, replica_groups=mesh['cell'=4,'chan'=8] {'cell'}, use_global_device_ids=true, to_apply=%region_7.9 | all-reduce | flops 1024 | bytes 8192 | tf_op jit(solution)/shard_map/psum | solution.py:39
  148.3 0.1 fusion.8
  148.4 0.1 copy.21
  148.5 2.9 %cholesky.81 = f32[32,32]{1,0:T(8,128)S(1)} custom-call(f32[32,32]{1,0:T(8,128)S(1)} %fusion.13), custom_call_target="Cholesky" | custom-call | tf_op jit(solution)/shard_map/jit(cholesky)/cholesky | solution.py:10
  151.4 0.6 compare_reduce_fusion
  152.1 0.0 all-reduce.5.cloned.1.call-update
  152.1 0.7 fusion.6
  152.7 0.0 copy-done.2
  152.8 2.4 %custom-call.25 = f32[1,32,32]{1,2,0:T(8,128)S(1)} custom-call(f32[1,32,32]{2,1,0:T(8,128)S(1)} %fusion.6), custom_call_target="InvertDiagBlocksLowerTriangular" | custom-call | tf_op jit(solution)/shard_map/jit(_cho_solve)/triangular_solve | solution.py:11
  155.2 38.6 %all-reduce.5.cloned.1.call-done = f32[32,1024]{1,0:T(8,128)} async-done(((f32[32,1024]{1,0:T(8,128)}), f32[32,1024]{1,0:T(8,128)}) %all-reduce.5.cloned.1.call-update) | async-done | bytes 131088 | tf_op jit(solution)/shard_map/psum | solution.py:42
  193.8 0.0 copy-done.9
  193.8 0.0 copy-done.6
  193.8 1.0 multiply_add_fusion.1
  194.8 0.0 copy-start.5
  194.8 0.3 fusion.11
  195.1 0.9 fusion.9
  196.1 0.0 copy-done
  196.1 0.0 copy-done.8
  196.1 0.0 copy-done.5
  (10 shorter events, 0.1 us)
Async XLA Ops:
  7.2 12.5 %copy-start.3 = (f32[32,1024]{1,0:T(8,128)S(1)}, f32[32,1024]{1,0:T(8,128)}, u32[]{:S(2)}) copy-start(f32[32,1024]{1,0:T(8,128)} %param.10) | copy-start | bytes 393220
  7.2 12.8 %copy-start.1 = (f32[32,8192]{1,0:T(8,128)S(1)}, f32[32,8192]{1,0:T(8,128)}, u32[]{:S(2)}) copy-start(f32[32,8192]{1,0:T(8,128)} %param.9) | copy-start | bytes 3145732
  7.2 104.3 %copy-start.10 = (f32[32,32]{1,0:T(8,128)S(1)}, f32[32,32]{1,0:T(8,128)}, u32[]{:S(2)}) copy-start(f32[32,32]{1,0:T(8,128)} %param.13) | copy-start | bytes 12292
  7.2 111.2 %copy-start.11 = (f32[32,32]{1,0:T(8,128)S(1)}, f32[32,32]{1,0:T(8,128)}, u32[]{:S(2)}) copy-start(f32[32,32]{1,0:T(8,128)} %param.14) | copy-start | bytes 12292
  7.2 111.3 %copy-start.4 = (f32[32,8192]{1,0:T(8,128)S(1)}, f32[32,8192]{1,0:T(8,128)}, u32[]{:S(2)}) copy-start(f32[32,8192]{1,0:T(8,128)} %param.11) | copy-start | bytes 3145732
  7.2 111.3 %all-reduce.3.cloned.1.call-start = ((), (), s32[]{:S(2)}) async-start(), calls=%async_computation | async-start | bytes 2097152 | tf_op jit(solution)/shard_map/psum | solution.py:35
  19.7 174.2 %all-reduce.5.cloned.1.call-start = ((), (), s32[]{:S(2)}) async-start(), calls=%async_computation.1 | async-start | bytes 262144 | tf_op jit(solution)/shard_map/psum | solution.py:42
  111.5 82.4 %copy-start.9 = (f32[32]{0:T(128)}, f32[32]{0:T(128)S(1)}, u32[]{:S(2)}) copy-start(f32[32]{0:T(128)S(1)} %convolution_bitcast_fusion) | copy-start | bytes 388
  111.7 20.7 %copy-start.7 = (f32[32,32]{1,0:T(8,128)}, f32[32,32]{1,0:T(8,128)S(1)}, u32[]{:S(2)}) copy-start(f32[32,32]{1,0:T(8,128)S(1)} %copy.18) | copy-start | bytes 12292
  119.9 32.8 %copy-start.2 = (f32[32,8192]{1,0:T(8,128)}, f32[32,8192]{1,0:T(8,128)S(1)}, u32[]{:S(2)}) copy-start(f32[32,8192]{1,0:T(8,128)S(1)} %multiply_add_fusion) | copy-start | bytes 3145732
  119.9 73.9 %copy-start.6 = (f32[32,1024]{1,0:T(8,128)S(1)}, f32[32,1024]{1,0:T(8,128)}, u32[]{:S(2)}) copy-start(f32[32,1024]{1,0:T(8,128)} %param.12) | copy-start | bytes 393220
  122.0 74.1 %copy-start = (f32[32,8192]{1,0:T(8,128)}, f32[32,8192]{1,0:T(8,128)S(1)}, u32[]{:S(2)}) copy-start(f32[32,8192]{1,0:T(8,128)S(1)} %fusion.14) | copy-start | bytes 3145732
  148.5 47.6 %copy-start.8 = (f32[32,32]{1,0:T(8,128)}, f32[32,32]{1,0:T(8,128)S(1)}, u32[]{:S(2)}) copy-start(f32[32,32]{1,0:T(8,128)S(1)} %copy.21) | copy-start | bytes 12292
  194.8 1.3 copy-start.5
Sparse Core Ops, SparseCore 0:
  19.8 61.7 all-reduce.2
  152.2 41.5 all-reduce.4
where the time goes:
time: 203 us
  blocking collectives  99.3 us (49%)
  waiting for transfers between devices  38.7 us (19%)
  matrix products  27.5 us (14%)
  other arithmetic  22.6 us (11%)
  between operations  14.3 us (7%)
    psum x1, waiting for transfers between devices, body(): cell_summed = lax.psum(slab_cell, 'cell')  38.6 us
    psum x1, blocking collectives, body(): rhs = lax.psum(rhs_part, ('cell', 'chan'))  37 us
    psum x1, blocking collectives, body(): chan_norm = lax.psum(chan_part, 'chan')  30.4 us
    psum x1, blocking collectives, body(): cell_norm = lax.psum(cell_part, 'cell')  16 us
    psum x1, blocking collectives, body(): new_norm = lax.psum(local_gram, 'cell')  15.9 us
    dot_general x1, matrix products, body(): lax.dot_general(chan_low, slab, (((1,), (1,)), ((), ())), preferred_eleme...  12.4 us
    another operation x9, other arithmetic, spd_solve(): lower = jnp.linalg.cholesky(matrix)  10.8 us
    dot_general x1, matrix products, body(): slab_cell = jnp.dot(cell_low, slab, preferred_element_type=jnp.float32)  9.41 us
  transfers between devices with their start and end apart: 2, of which 1 were waited for; matrix products, arithmetic and copies ran while one was open for 9% of the time, Pallas kernels for 0%

commit v1 on v0

v1 whole, which is shorter than its diff:
```python
import functools
import math

import jax
import jax.numpy as jnp
from jax import lax
from jax.experimental import pallas as pl
from jax.experimental.pallas import tpu as pltpu
from jax.sharding import PartitionSpec as P

CHUNKS = 4
STATS_CHUNK = 1
LANES = 128
HI = lax.Precision.HIGHEST
ROWS = (((1,), (1,)), ((), ()))
WHOLE = pl.BlockSpec(memory_space=pltpu.VMEM)
PARAMS = pltpu.CompilerParams(vmem_limit_bytes=44 << 20)


def eye(n):
    i = lax.broadcasted_iota(jnp.int32, (n, n), 0)
    j = lax.broadcasted_iota(jnp.int32, (n, n), 1)
    return (i == j).astype(jnp.float32)


def eliminate(aug, n):
    rows = lax.broadcasted_iota(jnp.int32, aug.shape, 0)
    for k in range(n):
        row = aug[k : k + 1, :] * (1.0 / aug[k : k + 1, k : k + 1])
        aug = jnp.where(rows == k, row, aug - aug[:, k : k + 1] * row)
    return aug[:, n:]


def pass_one(all_rows, all_cols, n_cell, n_chan, chan_ref, cell_ref, slab_ref, *refs):
    sends, keeps = refs[:CHUNKS], refs[CHUNKS : 2 * CHUNKS]
    stats_ref, slab_v, sem = refs[2 * CHUNKS :]
    core = lax.rem(lax.axis_index("chan"), 2)
    width = slab_ref.shape[0] // (2 * CHUNKS)
    jobs = []
    for k in range(CHUNKS):
        for half, out in ((1 - core, sends[k]), (core, keeps[k])):
            at = pl.ds(pl.multiple_of((2 * k + half) * width, width), width)
            copy = pltpu.make_async_copy(slab_ref.at[at], slab_v.at[at], sem.at[len(jobs)])
            copy.start()
            jobs.append((copy, at, out))
    chan = chan_ref[...]
    low = chan.astype(jnp.bfloat16)
    cell = cell_ref[...]
    chan_gram = lax.dot_general(chan, chan, ROWS, precision=HI) / (all_cols * n_cell)
    cell_gram = lax.dot_general(cell, cell, ROWS, precision=HI) / (all_rows * n_chan)
    total = jnp.zeros((chan.shape[0], LANES), jnp.float32)
    for copy, at, out in jobs:
        copy.wait()
        part = lax.dot_general(low, slab_v[at], ROWS, preferred_element_type=jnp.float32)
        out[...] = part
        part = part * cell_ref[:, at]
        for j in range(0, width, LANES):
            total += part[:, j : j + LANES]
    rhs = jnp.sum(total, axis=1, keepdims=True) / math.sqrt(all_rows * all_cols)
    pad = jnp.zeros((chan.shape[0], LANES - 1 - 2 * chan.shape[0]), jnp.float32)
    stats_ref[...] = jnp.concatenate([cell_gram, chan_gram, rhs, pad], axis=1)


def solve_one(stats_ref, acc_ref, row_ref, gram_ref, out_ref):
    stats = stats_ref[...]
    n = stats.shape[0]
    cell_norm, chan_norm, rhs = stats[:, :n], stats[:, n : 2 * n], stats[:, 2 * n : 2 * n + 1]
    time = eliminate(jnp.concatenate([cell_norm * chan_norm, rhs], axis=1), n)
    row = jnp.sum(eye(n) * time, axis=0, keepdims=True)
    outer = time * row
    gram = acc_ref[...] + chan_norm * outer
    inverse = eliminate(jnp.concatenate([gram, eye(n)], axis=1), n)
    row_ref[...] = row
    gram_ref[...] = gram
    pad = jnp.zeros((n, LANES - 2 * n - 1), jnp.float32)
    out_ref[...] = jnp.concatenate([inverse, outer, time, pad], axis=1)


def pass_two(all_rows, all_cols, solved_ref, mttkrp_ref, slab_v, *refs):
    own, other = refs[:CHUNKS], refs[CHUNKS : 2 * CHUNKS]
    new_mttkrp, new_factor, out_ref = refs[2 * CHUNKS :]
    n = solved_ref.shape[0]
    core = lax.rem(lax.axis_index("chan"), 2)
    width = slab_v.shape[0] // (2 * CHUNKS)
    cols = slab_v.shape[1]
    inverse = solved_ref[:, :n]
    time = solved_ref[:, 2 * n : 2 * n + 1] / math.sqrt(all_cols)
    total = jnp.zeros((n, cols), jnp.float32)
    gram = jnp.zeros((n, n), jnp.float32)
    for k in range(CHUNKS):
        for half, part in ((core, own[k]), (1 - core, other[k])):
            at = pl.ds(pl.multiple_of((2 * k + half) * width, width), width)
            right = mttkrp_ref[:, at] + time * part[:, :width]
            new_mttkrp[:, at] = right
            factor = jnp.dot(inverse, right, precision=HI)
            new_factor[:, at] = factor
            gram += lax.dot_general(factor, factor, ROWS, precision=HI)
            low = factor.astype(jnp.bfloat16)
            total += jnp.dot(low, slab_v[at], preferred_element_type=jnp.float32)
    out_ref[:, :cols] = total
    pad = jnp.zeros((n, LANES - n), jnp.float32)
    out_ref[:, cols:] = jnp.concatenate([gram / all_rows, pad], axis=1)


def solve_two(all_rows, n_parts, solved_ref, mttkrp_ref, acc_ref, *refs):
    parts = [r[...] for r in refs[:n_parts]]
    new_mttkrp, new_factor, new_gram = refs[n_parts:]
    while len(parts) > 1:
        parts = [a + b for a, b in zip(parts[::2], parts[1::2])]
    (summed,) = parts
    n, cols = mttkrp_ref.shape
    outer = solved_ref[:, n : 2 * n]
    time = solved_ref[:, 2 * n : 2 * n + 1] / math.sqrt(all_rows)
    gram = acc_ref[...] + summed[:, cols : cols + n] * outer
    inverse = eliminate(jnp.concatenate([gram, eye(n)], axis=1), n)
    right = mttkrp_ref[...] + time * summed[:, :cols]
    new_mttkrp[...] = right
    new_factor[...] = jnp.dot(inverse, right, precision=HI)
    new_gram[...] = gram


def over_cell(x, n_cell):
    masks = 1
    while masks < n_cell // 4:
        masks *= 2
        x = x + lax.ppermute(x, "cell", [(i, i ^ (2 * masks)) for i in range(n_cell)])
    near = [m for m in (1, 2, 3) if m < n_cell]
    return [x] + [lax.ppermute(x, "cell", [(i, i ^ m) for i in range(n_cell)]) for m in near]


def pair_sum(parts):
    while len(parts) > 1:
        parts = [a + b for a, b in zip(parts[::2], parts[1::2])]
    return parts[0]


def hop(x, moves):
    return lax.ppermute(x, "chan", [(2 * a + c, 2 * b + c) for a, b in moves for c in (0, 1)])


def over_chips(x, n_chip):
    chip = lax.axis_index("chan") // 2
    far = n_chip - 1
    half = n_chip // 2
    for s in range(half - 1):
        x = x + hop(x, [(s, s + 1), (far - s, far - s - 1)])
    x = x + hop(x, [(half - 1, half), (half, half - 1)])
    for s in reversed(range(half - 1)):
        got = hop(x, [(s + 1, s), (far - s - 1, far - s)])
        x = jnp.where((chip == s) | (chip == far - s), got, x)
    return x


def body(slab, cell_factor, chan_factor, cell_mttkrp, chan_mttkrp, cell_gram_acc, chan_gram_acc):
    n_cell = lax.axis_size("cell")
    n_chan = lax.axis_size("chan")
    rows, cols = slab.shape
    rank = cell_factor.shape[0]
    all_rows, all_cols = rows * n_cell, cols * n_chan
    width = rows // (2 * CHUNKS)
    f32 = functools.partial(jax.ShapeDtypeStruct, dtype=jnp.float32)

    first = pl.pallas_call(
        functools.partial(pass_one, all_rows, all_cols, n_cell, n_chan),
        in_specs=[WHOLE, WHOLE, pl.BlockSpec(memory_space=pl.ANY)],
        out_specs=[WHOLE] * (2 * CHUNKS + 2),
        out_shape=[f32((rank, width))] * (2 * CHUNKS)
        + [f32((rank, LANES)), pltpu.VMEM((rows, cols), slab.dtype)],
        scratch_shapes=[pltpu.SemaphoreType.DMA((2 * CHUNKS,))],
        compiler_params=PARAMS,
        name="pass_one",
    )(chan_factor, cell_factor, slab)
    sends, keeps = list(first[:CHUNKS]), list(first[CHUNKS : 2 * CHUNKS])
    stats, slab_v = first[2 * CHUNKS :]
    slab_v = pltpu.with_memory_space_constraint(slab_v, pltpu.VMEM)

    stats = pair_sum(over_cell(stats, n_cell))
    sends[STATS_CHUNK] = jnp.concatenate([sends[STATS_CHUNK], stats], axis=1)
    keeps[STATS_CHUNK] = jnp.concatenate([keeps[STATS_CHUNK], stats], axis=1)
    swap = [(i, i ^ 1) for i in range(n_chan)]
    own = [keep + lax.ppermute(send, "chan", swap) for send, keep in zip(sends, keeps)]
    own = [over_chips(x, n_chan // 2) for x in own]
    other = [lax.ppermute(x[:, :width], "chan", swap) for x in own]

    row, new_cell_gram, solved = pl.pallas_call(
        solve_one,
        in_specs=[WHOLE] * 2,
        out_specs=[WHOLE] * 3,
        out_shape=[f32((1, rank)), f32((rank, rank)), f32((rank, LANES))],
        name="solve_one",
    )(own[STATS_CHUNK][:, width:], cell_gram_acc)

    new_cell_mttkrp, new_cell_factor, part = pl.pallas_call(
        functools.partial(pass_two, all_rows, all_cols),
        in_specs=[WHOLE] * (3 + 2 * CHUNKS),
        out_specs=[WHOLE] * 3,
        out_shape=[f32((rank, rows)), f32((rank, rows)), f32((rank, cols + LANES))],
        compiler_params=PARAMS,
        name="pass_two",
    )(solved, cell_mttkrp, slab_v, *own, *other)

    parts = over_cell(part, n_cell)
    new_chan_mttkrp, new_chan_factor, new_chan_gram = pl.pallas_call(
        functools.partial(solve_two, all_rows, len(parts)),
        in_specs=[WHOLE] * (3 + len(parts)),
        out_specs=[WHOLE] * 3,
        out_shape=[f32((rank, cols)), f32((rank, cols)), f32((rank, rank))],
        name="solve_two",
    )(solved, chan_mttkrp, chan_gram_acc, *parts)
    return (
        row.reshape(rank),
        new_cell_factor,
        new_chan_factor,
        new_cell_mttkrp,
        new_chan_mttkrp,
        new_cell_gram,
        new_chan_gram,
    )


def solution(mesh):
    placed = (
        P("cell", "chan"),
        P(None, "cell"),
        P(None, "chan"),
        P(None, "cell"),
        P(None, "chan"),
        P(),
        P(),
    )
    return jax.shard_map(
        body,
        mesh=mesh,
        in_specs=placed,
        out_specs=(
            P(),
            P(None, "cell"),
            P(None, "chan"),
            P(None, "cell"),
            P(None, "chan"),
            P(),
            P(),
        ),
        check_vma=False,
    )
```

time: 203 us -> 103 us (0.51)
  blocking collectives: 99.3 us -> 0 us
  Pallas kernels: 0 us -> 29.1 us
  matrix products: 27.5 us -> 0 us
  starting transfers between devices: 0.08 us -> 24.7 us
  other arithmetic: 22.6 us -> 5.57 us
  local copies, waits for them, and re-layouts: 0.45 us -> 14.1 us
  between operations: 14.3 us -> 1.07 us
  waiting for transfers between devices: 38.7 us -> 27.9 us
    psum x4 -> x0, blocking collectives: 99.3 us -> none  [the longest x1 37 us: body(): rhs = lax.psum(rhs_part, ('cell', 'chan'))]
    psum x2 -> x0, waiting for transfers between devices: 38.6 us -> none  [the longest x1 38.6 us: body(): cell_summed = lax.psum(slab_cell, 'cell')]
    pallas_call x0 -> x4, Pallas kernels: none -> 29.1 us  [the longest x1 10.4 us: body(): pl.pallas_call(functools.partial(pass_one, all_rows, all_cols, n_cell, n_...]
    ppermute x0 -> x26, waiting for transfers between devices: none -> 27.9 us  [the longest x12 16.1 us: hop(): lax.ppermute(x, 'chan', [(2 * a + c, 2 * b + c) for a, b in moves for c i...]
    ppermute x0 -> x26, starting transfers between devices: none -> 24.7 us  [the longest x12 15.4 us: hop(): lax.ppermute(x, 'chan', [(2 * a + c, 2 * b + c) for a, b in moves for c i...]
    dot_general x5 -> x0, matrix products: 23.9 us -> none  [the longest x1 12.4 us: body(): lax.dot_general(chan_low, slab, (((1,), (1,)), ((), ())), preferred_eleme...]
    another operation x15 -> x0, other arithmetic: 20 us -> none  [the longest x9 10.8 us: spd_solve(): lower = jnp.linalg.cholesky(matrix)]
    unnamed x26, local copies, waits for them, and re-layouts: 0.23 us -> 13.5 us
  transfers between devices with their start and end apart: 2 -> 26, of which waited for: 1 -> 13; matrix products, arithmetic and copies ran while one was open for 9% -> 4% of each run, Pallas kernels for 0% -> 7%
where the time goes in v1:
time: 103 us; the launch traced here: 102 us
  Pallas kernels  29.1 us (28%)
  waiting for transfers between devices  27.9 us (27%)
  starting transfers between devices  24.7 us (24%)
  local copies, waits for them, and re-layouts  14.1 us (14%)
  other arithmetic  5.57 us (5%)
  between operations  1.07 us (1%)
    ppermute x12, waiting for transfers between devices, hop(): lax.ppermute(x, 'chan', [(2 * a + c, 2 * b + c) for a, b in moves for c i...  16.1 us
    ppermute x12, starting transfers between devices, hop(): lax.ppermute(x, 'chan', [(2 * a + c, 2 * b + c) for a, b in moves for c i...  15.4 us
    unnamed x26, local copies, waits for them, and re-layouts  13.5 us
    ppermute x6, waiting for transfers between devices, over_cell(): lax.ppermute(x, 'cell', [(i, i ^ m) for i in range(n_cell)])  11 us
    pallas_call x1, Pallas kernels, body(): pl.pallas_call(functools.partial(pass_one, all_rows, all_cols, n_cell, n_...  10.4 us
    ppermute x6, starting transfers between devices, over_cell(): lax.ppermute(x, 'cell', [(i, i ^ m) for i in range(n_cell)])  7.95 us
    pallas_call x1, Pallas kernels, body(): pl.pallas_call(solve_one, in_specs=[WHOLE] * 2, out_specs=[WHOLE] * 3, ou...  7.08 us
    pallas_call x1, Pallas kernels, body(): pl.pallas_call(functools.partial(pass_two, all_rows, all_cols), in_specs=...  6.72 us
  transfers between devices with their start and end apart: 26, of which 13 were waited for; matrix products, arithmetic and copies ran while one was open for 4% of the time, Pallas kernels for 7%

profile of v1, /device:TPU:0, one launch (start us, length us, event | category | flops | bytes accessed | tf_op | source)
XLA Modules:
  0.0 102.4 jit_solution(1721995843553713371)
XLA Ops:
  0.6 10.4 %pass_one.1 = (f32[32,1024]{1,0:T(8,128)}, f32[32,1024]{1,0:T(8,128)}, f32[32,1024]{1,0:T(8,128)}, f32[32,1024]{1,0:T(8,128)}, f32[32,1024]{1,0:T(8,128)}, /*ind...) custom-call(f32[32,1024]{1,0:T(8,128)} %chan_ref.1, ...), custom_call_target="tpu_custom_call" | custom-call | tf_op jit(solution)/shard_map/pass_one/pallas_call | solution.py:163
  11.0 5.7 %copy-done = bf16[8192,1024]{1,0:T(8,128)(2,1)} copy-done((bf16[8192,1024]{1,0:T(8,128)(2,1)}, bf16[8192,1024]{1,0:T(8,128)(2,1)S(1)}, u32[]{:S(2)}) %copy-start) | copy-done | bytes 16777240
  16.8 3.9 %collective-permute-start.2 = (f32[32,128]{1,0:T(8,128)}, f32[32,128]{1,0:T(8,128)S(1)}, u32[]{:S(2)}, u32[]{:S(2)}) collective-permute-start(f32[32,128]{1,0:T(8,128)} %get-tuple-element.27), channel_id=1, source_target_pairs={{0,24},{8,16},{16,8},{24,0},{1,25},{9,17},{17,9},{25,1},{2,26},{10... | collective-permute-start | bytes 49160 | tf_op jit(solution)/shard_map/ppermute | solution.py:128
  20.7 0.5 collective-permute-start.1
  21.2 0.1 collective-permute-start
  21.2 1.4 %collective-permute-done.2 = f32[32,128]{1,0:T(8,128)S(1)} collective-permute-done((f32[32,128]{1,0:T(8,128)}, f32[32,128]{1,0:T(8,128)S(1)}, u32[]{:S(2)}, u32[]{:S(2)}) %collective-permute-start.2) | collective-permute-done | bytes 16416 | tf_op jit(solution)/shard_map/ppermute | solution.py:128
  22.6 2.0 %collective-permute-done.1 = f32[32,128]{1,0:T(8,128)S(1)} collective-permute-done((f32[32,128]{1,0:T(8,128)}, f32[32,128]{1,0:T(8,128)S(1)}, u32[]{:S(2)}, u32[]{:S(2)}) %collective-permute-start.1) | collective-permute-done | bytes 16416 | tf_op jit(solution)/shard_map/ppermute | solution.py:128
  24.6 0.5 collective-permute-done
  25.1 0.7 add_add_fusion
  25.9 0.9 pad_maximum_fusion
  26.8 0.1 collective-permute-start.3
  26.9 0.5 collective-permute-start.7
  27.4 0.1 collective-permute-start.11
  27.4 0.4 collective-permute-start.15
  27.9 0.7 collective-permute-done.7
  28.6 0.9 add.52
  29.5 3.5 %collective-permute-start.8 = (f32[32,1024]{1,0:T(8,128)S(1)}, f32[32,1024]{1,0:T(8,128)S(1)}, u32[]{:S(2)}, u32[]{:S(2)}) collective-permute-start(f32[32,1024]{1,0:T(8,128)S(1)} %add.52), channel_id=1, source_target_pairs={{0,2},{1,3},{6,4},{7,5},{8,10},{9,11},{14,12},{15,13},{16,18},{17,... | collective-permute-start | bytes 393224 | tf_op jit(solution)/shard_map/ppermute | solution.py:138
  33.0 0.9 fusion
  34.0 1.3 %collective-permute-start.4 = (f32[32,1152]{1,0:T(8,128)S(1)}, f32[32,1152]{1,0:T(8,128)S(1)}, u32[]{:S(2)}, u32[]{:S(2)}) collective-permute-start(f32[32,1152]{1,0:T(8,128)S(1)} %fusion), channel_id=1, source_target_pairs={{0,2},{1,3},{6,4},{7,5},{8,10},{9,11},{14,12},{15,13},{16,18},{17,... | collective-permute-start | bytes 442376 | tf_op jit(solution)/shard_map/ppermute | solution.py:138
  35.3 0.0 collective-permute-done.11
  35.3 0.9 add.55
  36.2 1.3 %collective-permute-start.12 = (f32[32,1024]{1,0:T(8,128)S(1)}, f32[32,1024]{1,0:T(8,128)S(1)}, u32[]{:S(2)}, u32[]{:S(2)}) collective-permute-start(f32[32,1024]{1,0:T(8,128)S(1)} %add.55), channel_id=1, source_target_pairs={{0,2},{1,3},{6,4},{7,5},{8,10},{9,11},{14,12},{15,13},{16,18},{17,... | collective-permute-start | bytes 393224 | tf_op jit(solution)/shard_map/ppermute | solution.py:138
  37.5 0.0 collective-permute-done.15
  37.5 0.9 add.58
  38.5 1.3 %collective-permute-start.16 = (f32[32,1024]{1,0:T(8,128)S(1)}, f32[32,1024]{1,0:T(8,128)S(1)}, u32[]{:S(2)}, u32[]{:S(2)}) collective-permute-start(f32[32,1024]{1,0:T(8,128)S(1)} %add.58), channel_id=1, source_target_pairs={{0,2},{1,3},{6,4},{7,5},{8,10},{9,11},{14,12},{15,13},{16,18},{17,... | collective-permute-start | bytes 393224 | tf_op jit(solution)/shard_map/ppermute | solution.py:138
  39.8 0.7 collective-permute-start.9
  40.5 0.0 collective-permute-done.4
  40.5 0.7 collective-permute-start.5
  41.2 1.5 %collective-permute-done.12 = f32[32,1024]{1,0:T(8,128)S(1)} collective-permute-done((f32[32,1024]{1,0:T(8,128)S(1)}, f32[32,1024]{1,0:T(8,128)S(1)}, u32[]{:S(2)}, u32[]{:S(2)}) %collective-permute-start.12) | collective-permute-done | bytes 131104 | tf_op jit(solution)/shard_map/ppermute | solution.py:138
  42.7 0.7 collective-permute-start.13
  43.4 1.6 %collective-permute-done.16 = f32[32,1024]{1,0:T(8,128)S(1)} collective-permute-done((f32[32,1024]{1,0:T(8,128)S(1)}, f32[32,1024]{1,0:T(8,128)S(1)}, u32[]{:S(2)}, u32[]{:S(2)}) %collective-permute-start.16) | collective-permute-done | bytes 131104 | tf_op jit(solution)/shard_map/ppermute | solution.py:138
  45.0 0.7 collective-permute-start.17
  45.7 1.3 %collective-permute-start.10 = (f32[32,1024]{1,0:T(8,128)S(1)}, f32[32,1024]{1,0:T(8,128)S(1)}, u32[]{:S(2)}, u32[]{:S(2)}) collective-permute-start(f32[32,1024]{1,0:T(8,128)S(1)} %add.54), channel_id=1, source_target_pairs={{2,0},{3,1},{4,6},{5,7},{10,8},{11,9},{12,14},{13,15},{18,16},{19,... | collective-permute-start | bytes 393224 | tf_op jit(solution)/shard_map/ppermute | solution.py:138
  47.1 1.3 %collective-permute-start.14 = (f32[32,1024]{1,0:T(8,128)S(1)}, f32[32,1024]{1,0:T(8,128)S(1)}, u32[]{:S(2)}, u32[]{:S(2)}) collective-permute-start(f32[32,1024]{1,0:T(8,128)S(1)} %add.57), channel_id=1, source_target_pairs={{2,0},{3,1},{4,6},{5,7},{10,8},{11,9},{12,14},{13,15},{18,16},{19,... | collective-permute-start | bytes 393224 | tf_op jit(solution)/shard_map/ppermute | solution.py:138
  48.4 0.0 collective-permute-done.17
  48.4 1.3 %collective-permute-start.18 = (f32[32,1024]{1,0:T(8,128)S(1)}, f32[32,1024]{1,0:T(8,128)S(1)}, u32[]{:S(2)}, u32[]{:S(2)}) collective-permute-start(f32[32,1024]{1,0:T(8,128)S(1)} %add.60), channel_id=1, source_target_pairs={{2,0},{3,1},{4,6},{5,7},{10,8},{11,9},{12,14},{13,15},{18,16},{19,... | collective-permute-start | bytes 393224 | tf_op jit(solution)/shard_map/ppermute | solution.py:138
  49.8 1.5 %collective-permute-start.6 = (f32[32,1152]{1,0:T(8,128)S(1)}, f32[32,1152]{1,0:T(8,128)S(1)}, u32[]{:S(2)}, u32[]{:S(2)}) collective-permute-start(f32[32,1152]{1,0:T(8,128)S(1)} %add.51), channel_id=1, source_target_pairs={{2,0},{3,1},{4,6},{5,7},{10,8},{11,9},{12,14},{13,15},{18,16},{19,... | collective-permute-start | bytes 442376 | tf_op jit(solution)/shard_map/ppermute | solution.py:138
  51.2 5.9 %collective-permute-done.10 = f32[32,1024]{1,0:T(8,128)S(1)} collective-permute-done((f32[32,1024]{1,0:T(8,128)S(1)}, f32[32,1024]{1,0:T(8,128)S(1)}, u32[]{:S(2)}, u32[]{:S(2)}) %collective-permute-start.10) | collective-permute-done | bytes 131104 | tf_op jit(solution)/shard_map/ppermute | solution.py:138
  57.2 0.0 copy-start.3
  57.2 0.1 collective-permute-start.19
  57.3 2.6 %collective-permute-done.14 = f32[32,1024]{1,0:T(8,128)S(1)} collective-permute-done((f32[32,1024]{1,0:T(8,128)S(1)}, f32[32,1024]{1,0:T(8,128)S(1)}, u32[]{:S(2)}, u32[]{:S(2)}) %collective-permute-start.14) | collective-permute-done | bytes 131104 | tf_op jit(solution)/shard_map/ppermute | solution.py:138
  59.9 0.0 copy-start.4
  59.9 0.1 collective-permute-start.21
  60.0 2.7 %collective-permute-done.18 = f32[32,1024]{1,0:T(8,128)S(1)} collective-permute-done((f32[32,1024]{1,0:T(8,128)S(1)}, f32[32,1024]{1,0:T(8,128)S(1)}, u32[]{:S(2)}, u32[]{:S(2)}) %collective-permute-start.18) | collective-permute-done | bytes 131104 | tf_op jit(solution)/shard_map/ppermute | solution.py:138
  62.7 0.1 collective-permute-start.22
  62.8 1.7 %collective-permute-done.6 = f32[32,1152]{1,0:T(8,128)S(1)} collective-permute-done((f32[32,1152]{1,0:T(8,128)S(1)}, f32[32,1152]{1,0:T(8,128)S(1)}, u32[]{:S(2)}, u32[]{:S(2)}) %collective-permute-start.6) | collective-permute-done | bytes 147488 | tf_op jit(solution)/shard_map/ppermute | solution.py:138
  64.6 0.1 collective-permute-start.20
  64.7 0.6 slice.8.stats_ref
  65.3 7.1 %solve_one.1 = (f32[1,32]{1,0:T(1,128)}, f32[32,32]{1,0:T(8,128)}, f32[32,128]{1,0:T(8,128)}) custom-call(f32[32,128]{1,0:T(8,128)} %slice.8.stats_ref, f32[32,32]{1,0:T(8,128)} %acc_ref.2), custom_call_target="tpu_custom_call" | custom-call | tf_op jit(solution)/shard_map/solve_one/pallas_call | solution.py:185
  72.4 0.6 copy-done.9
  73.0 0.1 copy-done.10
  73.1 0.1 copy-done.11
  73.1 0.1 copy-done.12
  73.2 5.8 %copy-done.1 = bf16[8192,1024]{1,0:T(8,128)(2,1)S(1)} copy-done((bf16[8192,1024]{1,0:T(8,128)(2,1)S(1)}, bf16[8192,1024]{1,0:T(8,128)(2,1)}, u32[]{:S(2)}) %copy-start.1) | copy-done | bytes 16777240
  78.9 6.7 %pass_two.1 = (f32[32,8192]{1,0:T(8,128)}, f32[32,8192]{1,0:T(8,128)}, f32[32,1152]{1,0:T(8,128)}) custom-call(f32[32,128]{1,0:T(8,128)} %get-tuple-element.30.solved_ref, f32[32,8192]{1,0:T(8,128)} %mttkrp_ref.2, bf16[8192,1024]{1,0:T(8,128)(2,1)S(1)} %copy-done.1, f32[32,1024]{1,0:T(8,128)} %copy-done.3, f32[32,1152]{1,0:T(8,128)} %copy-done.2, ...), custom_call_target="tpu_custom_call" | custom-call | tf_op jit(solution)/shard_map/pass_two/pallas_call | solution.py:193
  85.7 1.5 %collective-permute-start.25 = (f32[32,1152]{1,0:T(8,128)}, f32[32,1152]{1,0:T(8,128)S(1)}, u32[]{:S(2)}, u32[]{:S(2)}) collective-permute-start(f32[32,1152]{1,0:T(8,128)} %get-tuple-element.39.refs_0_), channel_id=1, source_target_pairs={{0,24},{8,16},{16,8},{24,0},{1,25},{9,17},{17,9},{25,1},{2,26},{10... | collective-permute-start | bytes 442376 | tf_op jit(solution)/shard_map/ppermute | solution.py:128
  87.2 0.5 collective-permute-start.24
  87.7 1.5 %collective-permute-start.23 = (f32[32,1152]{1,0:T(8,128)}, f32[32,1152]{1,0:T(8,128)S(1)}, u32[]{:S(2)}, u32[]{:S(2)}) collective-permute-start(f32[32,1152]{1,0:T(8,128)} %get-tuple-element.39.refs_0_), channel_id=1, source_target_pairs={{0,8},{8,0},{16,24},{24,16},{1,9},{9,1},{17,25},{25,17},{2,10},{10... | collective-permute-start | bytes 442376 | tf_op jit(solution)/shard_map/ppermute | solution.py:128
  89.2 4.3 %collective-permute-done.25.refs_3_ = f32[32,1152]{1,0:T(8,128)S(1)} collective-permute-done((f32[32,1152]{1,0:T(8,128)}, f32[32,1152]{1,0:T(8,128)S(1)}, u32[]{:S(2)}, u32[]{:S(2)}) %collective-permute-start.25) | collective-permute-done | bytes 147488 | tf_op jit(solution)/shard_map/ppermute | solution.py:128
  93.5 2.7 %collective-permute-done.24.refs_2_ = f32[32,1152]{1,0:T(8,128)S(1)} collective-permute-done((f32[32,1152]{1,0:T(8,128)}, f32[32,1152]{1,0:T(8,128)S(1)}, u32[]{:S(2)}, u32[]{:S(2)}) %collective-permute-start.24) | collective-permute-done | bytes 147488 | tf_op jit(solution)/shard_map/ppermute | solution.py:128
  96.2 0.1 collective-permute-done.23.refs_1_
  96.3 0.6 copy-done.7
  96.8 0.7 copy-done.8
  97.5 5.0 %solve_two.1 = (f32[32,1024]{1,0:T(8,128)}, f32[32,1024]{1,0:T(8,128)}, f32[32,32]{1,0:T(8,128)}) custom-call(f32[32,128]{1,0:T(8,128)} %get-tuple-element.30.solved_ref, f32[32,1024]{1,0:T(8,128)} %mttkrp_ref.3, f32[32,32]{1,0:T(8,128)} %acc_ref.3, f32[32,1152]{1,0:T(8,128)} %get-tuple-element.39.refs_0_, f32[32,1152]{1,0:T(8,128)} %copy-done.8, ...), custom_call_target="tpu_custom_call" | custom-call | tf_op jit(solution)/shard_map/solve_two/pallas_call | solution.py:203
  (38 shorter events, 0.3 us)
Async XLA Ops:
  11.0 5.8 %copy-start = (bf16[8192,1024]{1,0:T(8,128)(2,1)}, bf16[8192,1024]{1,0:T(8,128)(2,1)S(1)}, u32[]{:S(2)}) copy-start(bf16[8192,1024]{1,0:T(8,128)(2,1)S(1)} %get-tuple-element.31.slab_v) | copy-start | bytes 50331652
  16.8 5.8 %collective-permute-start.2 = (f32[32,128]{1,0:T(8,128)}, f32[32,128]{1,0:T(8,128)S(1)}, u32[]{:S(2)}, u32[]{:S(2)}) collective-permute-start(f32[32,128]{1,0:T(8,128)} %get-tuple-element.27), channel_id=1, source_target_pairs={{0,24},{8,16},{16,8},{24,0},{1,25},{9,17},{17,9},{25,1},{2,26},{10... | collective-permute-start | bytes 49160 | tf_op jit(solution)/shard_map/ppermute | solution.py:128
  20.7 3.9 %collective-permute-start.1 = (f32[32,128]{1,0:T(8,128)}, f32[32,128]{1,0:T(8,128)S(1)}, u32[]{:S(2)}, u32[]{:S(2)}) collective-permute-start(f32[32,128]{1,0:T(8,128)} %get-tuple-element.27), channel_id=1, source_target_pairs={{0,16},{8,24},{16,0},{24,8},{1,17},{9,25},{17,1},{25,9},{2,18},{10... | collective-permute-start | bytes 49160 | tf_op jit(solution)/shard_map/ppermute | solution.py:128
  21.2 3.9 %collective-permute-start = (f32[32,128]{1,0:T(8,128)}, f32[32,128]{1,0:T(8,128)S(1)}, u32[]{:S(2)}, u32[]{:S(2)}) collective-permute-start(f32[32,128]{1,0:T(8,128)} %get-tuple-element.27), channel_id=1, source_target_pairs={{0,8},{8,0},{16,24},{24,16},{1,9},{9,1},{17,25},{25,17},{2,10},{10... | collective-permute-start | bytes 49160 | tf_op jit(solution)/shard_map/ppermute | solution.py:128
  26.8 6.3 %collective-permute-start.3 = (f32[32,1152]{1,0:T(8,128)S(1)}, f32[32,1152]{1,0:T(8,128)S(1)}, u32[]{:S(2)}, u32[]{:S(2)}) collective-permute-start(f32[32,1152]{1,0:T(8,128)S(1)} %pad_maximum_fusion), channel_id=1, source_target_pairs={{0,1},{1,0},{2,3},{3,2},{4,5},{5,4},{6,7},{7,6},{8,9},{9,8},{10,11... | collective-permute-start | bytes 442376 | tf_op jit(solution)/shard_map/ppermute | solution.py:181
  26.9 1.8 %collective-permute-start.7 = (f32[32,1024]{1,0:T(8,128)}, f32[32,1024]{1,0:T(8,128)S(1)}, u32[]{:S(2)}, u32[]{:S(2)}) collective-permute-start(f32[32,1024]{1,0:T(8,128)} %get-tuple-element.33), channel_id=1, source_target_pairs={{0,1},{1,0},{2,3},{3,2},{4,5},{5,4},{6,7},{7,6},{8,9},{9,8},{10,11... | collective-permute-start | bytes 393224 | tf_op jit(solution)/shard_map/ppermute | solution.py:181
  27.4 7.9 %collective-permute-start.11 = (f32[32,1024]{1,0:T(8,128)}, f32[32,1024]{1,0:T(8,128)S(1)}, u32[]{:S(2)}, u32[]{:S(2)}) collective-permute-start(f32[32,1024]{1,0:T(8,128)} %get-tuple-element.35), channel_id=1, source_target_pairs={{0,1},{1,0},{2,3},{3,2},{4,5},{5,4},{6,7},{7,6},{8,9},{9,8},{10,11... | collective-permute-start | bytes 393224 | tf_op jit(solution)/shard_map/ppermute | solution.py:181
  27.4 10.1 %collective-permute-start.15 = (f32[32,1024]{1,0:T(8,128)}, f32[32,1024]{1,0:T(8,128)S(1)}, u32[]{:S(2)}, u32[]{:S(2)}) collective-permute-start(f32[32,1024]{1,0:T(8,128)} %get-tuple-element.37), channel_id=1, source_target_pairs={{0,1},{1,0},{2,3},{3,2},{4,5},{5,4},{6,7},{7,6},{8,9},{9,8},{10,11... | collective-permute-start | bytes 393224 | tf_op jit(solution)/shard_map/ppermute | solution.py:181
  29.5 10.2 %collective-permute-start.8 = (f32[32,1024]{1,0:T(8,128)S(1)}, f32[32,1024]{1,0:T(8,128)S(1)}, u32[]{:S(2)}, u32[]{:S(2)}) collective-permute-start(f32[32,1024]{1,0:T(8,128)S(1)} %add.52), channel_id=1, source_target_pairs={{0,2},{1,3},{6,4},{7,5},{8,10},{9,11},{14,12},{15,13},{16,18},{17,... | collective-permute-start | bytes 393224 | tf_op jit(solution)/shard_map/ppermute | solution.py:138
  34.0 6.5 %collective-permute-start.4 = (f32[32,1152]{1,0:T(8,128)S(1)}, f32[32,1152]{1,0:T(8,128)S(1)}, u32[]{:S(2)}, u32[]{:S(2)}) collective-permute-start(f32[32,1152]{1,0:T(8,128)S(1)} %fusion), channel_id=1, source_target_pairs={{0,2},{1,3},{6,4},{7,5},{8,10},{9,11},{14,12},{15,13},{16,18},{17,... | collective-permute-start | bytes 442376 | tf_op jit(solution)/shard_map/ppermute | solution.py:138
  36.2 6.5 %collective-permute-start.12 = (f32[32,1024]{1,0:T(8,128)S(1)}, f32[32,1024]{1,0:T(8,128)S(1)}, u32[]{:S(2)}, u32[]{:S(2)}) collective-permute-start(f32[32,1024]{1,0:T(8,128)S(1)} %add.55), channel_id=1, source_target_pairs={{0,2},{1,3},{6,4},{7,5},{8,10},{9,11},{14,12},{15,13},{16,18},{17,... | collective-permute-start | bytes 393224 | tf_op jit(solution)/shard_map/ppermute | solution.py:138
  38.5 6.5 %collective-permute-start.16 = (f32[32,1024]{1,0:T(8,128)S(1)}, f32[32,1024]{1,0:T(8,128)S(1)}, u32[]{:S(2)}, u32[]{:S(2)}) collective-permute-start(f32[32,1024]{1,0:T(8,128)S(1)} %add.58), channel_id=1, source_target_pairs={{0,2},{1,3},{6,4},{7,5},{8,10},{9,11},{14,12},{15,13},{16,18},{17,... | collective-permute-start | bytes 393224 | tf_op jit(solution)/shard_map/ppermute | solution.py:138
  39.8 5.9 %collective-permute-start.9 = (f32[32,1024]{1,0:T(8,128)S(1)}, f32[32,1024]{1,0:T(8,128)S(1)}, u32[]{:S(2)}, u32[]{:S(2)}) collective-permute-start(f32[32,1024]{1,0:T(8,128)S(1)} %add.53), channel_id=1, source_target_pairs={{2,4},{3,5},{4,2},{5,3},{10,12},{11,13},{12,10},{13,11},{18,20},{1... | collective-permute-start | bytes 393224 | tf_op jit(solution)/shard_map/ppermute | solution.py:138
  40.5 9.2 %collective-permute-start.5 = (f32[32,1152]{1,0:T(8,128)S(1)}, f32[32,1152]{1,0:T(8,128)S(1)}, u32[]{:S(2)}, u32[]{:S(2)}) collective-permute-start(f32[32,1152]{1,0:T(8,128)S(1)} %add.50), channel_id=1, source_target_pairs={{2,4},{3,5},{4,2},{5,3},{10,12},{11,13},{12,10},{13,11},{18,20},{1... | collective-permute-start | bytes 442376 | tf_op jit(solution)/shard_map/ppermute | solution.py:138
  42.7 4.3 %collective-permute-start.13 = (f32[32,1024]{1,0:T(8,128)S(1)}, f32[32,1024]{1,0:T(8,128)S(1)}, u32[]{:S(2)}, u32[]{:S(2)}) collective-permute-start(f32[32,1024]{1,0:T(8,128)S(1)} %add.56), channel_id=1, source_target_pairs={{2,4},{3,5},{4,2},{5,3},{10,12},{11,13},{12,10},{13,11},{18,20},{1... | collective-permute-start | bytes 393224 | tf_op jit(solution)/shard_map/ppermute | solution.py:138
  45.0 3.4 %collective-permute-start.17 = (f32[32,1024]{1,0:T(8,128)S(1)}, f32[32,1024]{1,0:T(8,128)S(1)}, u32[]{:S(2)}, u32[]{:S(2)}) collective-permute-start(f32[32,1024]{1,0:T(8,128)S(1)} %add.59), channel_id=1, source_target_pairs={{2,4},{3,5},{4,2},{5,3},{10,12},{11,13},{12,10},{13,11},{18,20},{1... | collective-permute-start | bytes 393224 | tf_op jit(solution)/shard_map/ppermute | solution.py:138
  45.7 11.4 %collective-permute-start.10 = (f32[32,1024]{1,0:T(8,128)S(1)}, f32[32,1024]{1,0:T(8,128)S(1)}, u32[]{:S(2)}, u32[]{:S(2)}) collective-permute-start(f32[32,1024]{1,0:T(8,128)S(1)} %add.54), channel_id=1, source_target_pairs={{2,0},{3,1},{4,6},{5,7},{10,8},{11,9},{12,14},{13,15},{18,16},{19,... | collective-permute-start | bytes 393224 | tf_op jit(solution)/shard_map/ppermute | solution.py:138
  47.1 12.8 %collective-permute-start.14 = (f32[32,1024]{1,0:T(8,128)S(1)}, f32[32,1024]{1,0:T(8,128)S(1)}, u32[]{:S(2)}, u32[]{:S(2)}) collective-permute-start(f32[32,1024]{1,0:T(8,128)S(1)} %add.57), channel_id=1, source_target_pairs={{2,0},{3,1},{4,6},{5,7},{10,8},{11,9},{12,14},{13,15},{18,16},{19,... | collective-permute-start | bytes 393224 | tf_op jit(solution)/shard_map/ppermute | solution.py:138
  48.4 14.3 %collective-permute-start.18 = (f32[32,1024]{1,0:T(8,128)S(1)}, f32[32,1024]{1,0:T(8,128)S(1)}, u32[]{:S(2)}, u32[]{:S(2)}) collective-permute-start(f32[32,1024]{1,0:T(8,128)S(1)} %add.60), channel_id=1, source_target_pairs={{2,0},{3,1},{4,6},{5,7},{10,8},{11,9},{12,14},{13,15},{18,16},{19,... | collective-permute-start | bytes 393224 | tf_op jit(solution)/shard_map/ppermute | solution.py:138
  49.8 14.8 %collective-permute-start.6 = (f32[32,1152]{1,0:T(8,128)S(1)}, f32[32,1152]{1,0:T(8,128)S(1)}, u32[]{:S(2)}, u32[]{:S(2)}) collective-permute-start(f32[32,1152]{1,0:T(8,128)S(1)} %add.51), channel_id=1, source_target_pairs={{2,0},{3,1},{4,6},{5,7},{10,8},{11,9},{12,14},{13,15},{18,16},{19,... | collective-permute-start | bytes 442376 | tf_op jit(solution)/shard_map/ppermute | solution.py:138
  57.2 15.2 %copy-start.3 = (f32[32,1024]{1,0:T(8,128)}, f32[32,1024]{1,0:T(8,128)S(1)}, u32[]{:S(2)}) copy-start(f32[32,1024]{1,0:T(8,128)S(1)} %broadcast_select_fusion.3.refs_0_) | copy-start | bytes 393220
  57.2 15.2 %collective-permute-start.19 = (f32[32,1024]{1,0:T(8,128)S(1)}, f32[32,1024]{1,0:T(8,128)S(1)}, u32[]{:S(2)}, u32[]{:S(2)}) collective-permute-start(f32[32,1024]{1,0:T(8,128)S(1)} %broadcast_select_fusion.3.refs_0_), channel_id=1, source_target_pairs={{0,1},{1,0},{2,3},{3,2},{4,5},{5,4},{6,7},{7,6},{8,9},{9,8},{10,11... | collective-permute-start | bytes 393224 | tf_op jit(solution)/shard_map/ppermute | solution.py:183
  59.9 12.5 %copy-start.4 = (f32[32,1024]{1,0:T(8,128)}, f32[32,1024]{1,0:T(8,128)S(1)}, u32[]{:S(2)}) copy-start(f32[32,1024]{1,0:T(8,128)S(1)} %broadcast_select_fusion.2.refs_2_) | copy-start | bytes 393220
  59.9 12.4 %collective-permute-start.21 = (f32[32,1024]{1,0:T(8,128)S(1)}, f32[32,1024]{1,0:T(8,128)S(1)}, u32[]{:S(2)}, u32[]{:S(2)}) collective-permute-start(f32[32,1024]{1,0:T(8,128)S(1)} %broadcast_select_fusion.2.refs_2_), channel_id=1, source_target_pairs={{0,1},{1,0},{2,3},{3,2},{4,5},{5,4},{6,7},{7,6},{8,9},{9,8},{10,11... | collective-permute-start | bytes 393224 | tf_op jit(solution)/shard_map/ppermute | solution.py:183
  62.7 9.7 %copy-start.5 = (f32[32,1024]{1,0:T(8,128)}, f32[32,1024]{1,0:T(8,128)S(1)}, u32[]{:S(2)}) copy-start(f32[32,1024]{1,0:T(8,128)S(1)} %broadcast_select_fusion.1.refs_3_) | copy-start | bytes 393220
  62.7 9.6 %collective-permute-start.22 = (f32[32,1024]{1,0:T(8,128)S(1)}, f32[32,1024]{1,0:T(8,128)S(1)}, u32[]{:S(2)}, u32[]{:S(2)}) collective-permute-start(f32[32,1024]{1,0:T(8,128)S(1)} %broadcast_select_fusion.1.refs_3_), channel_id=1, source_target_pairs={{0,1},{1,0},{2,3},{3,2},{4,5},{5,4},{6,7},{7,6},{8,9},{9,8},{10,11... | collective-permute-start | bytes 393224 | tf_op jit(solution)/shard_map/ppermute | solution.py:183
  64.6 7.9 %copy-start.2 = (f32[32,1152]{1,0:T(8,128)}, f32[32,1152]{1,0:T(8,128)S(1)}, u32[]{:S(2)}) copy-start(f32[32,1152]{1,0:T(8,128)S(1)} %broadcast_select_fusion.refs_1_) | copy-start | bytes 442372
  64.6 7.8 %collective-permute-start.20 = (f32[32,1024]{1,0:T(8,128)S(1)}, f32[32,1024]{1,0:T(8,128)S(1)}, u32[]{:S(2)}, u32[]{:S(2)}) collective-permute-start(f32[32,1024]{1,0:T(8,128)S(1)} %slice.9), channel_id=1, source_target_pairs={{0,1},{1,0},{2,3},{3,2},{4,5},{5,4},{6,7},{7,6},{8,9},{9,8},{10,11... | collective-permute-start | bytes 393224 | tf_op jit(solution)/shard_map/ppermute | solution.py:183
  72.3 0.7 copy-start.9
  72.4 0.7 copy-start.10
  72.4 0.7 copy-start.11
  72.4 0.8 copy-start.12
  73.2 5.8 %copy-start.1 = (bf16[8192,1024]{1,0:T(8,128)(2,1)S(1)}, bf16[8192,1024]{1,0:T(8,128)(2,1)}, u32[]{:S(2)}) copy-start(bf16[8192,1024]{1,0:T(8,128)(2,1)} %copy-done) | copy-start | bytes 50331652
  85.7 7.8 %collective-permute-start.25 = (f32[32,1152]{1,0:T(8,128)}, f32[32,1152]{1,0:T(8,128)S(1)}, u32[]{:S(2)}, u32[]{:S(2)}) collective-permute-start(f32[32,1152]{1,0:T(8,128)} %get-tuple-element.39.refs_0_), channel_id=1, source_target_pairs={{0,24},{8,16},{16,8},{24,0},{1,25},{9,17},{17,9},{25,1},{2,26},{10... | collective-permute-start | bytes 442376 | tf_op jit(solution)/shard_map/ppermute | solution.py:128
  87.2 9.0 %collective-permute-start.24 = (f32[32,1152]{1,0:T(8,128)}, f32[32,1152]{1,0:T(8,128)S(1)}, u32[]{:S(2)}, u32[]{:S(2)}) collective-permute-start(f32[32,1152]{1,0:T(8,128)} %get-tuple-element.39.refs_0_), channel_id=1, source_target_pairs={{0,16},{8,24},{16,0},{24,8},{1,17},{9,25},{17,1},{25,9},{2,18},{10... | collective-permute-start | bytes 442376 | tf_op jit(solution)/shard_map/ppermute | solution.py:128
  87.7 8.6 %collective-permute-start.23 = (f32[32,1152]{1,0:T(8,128)}, f32[32,1152]{1,0:T(8,128)S(1)}, u32[]{:S(2)}, u32[]{:S(2)}) collective-permute-start(f32[32,1152]{1,0:T(8,128)} %get-tuple-element.39.refs_0_), channel_id=1, source_target_pairs={{0,8},{8,0},{16,24},{24,16},{1,9},{9,1},{17,25},{25,17},{2,10},{10... | collective-permute-start | bytes 442376 | tf_op jit(solution)/shard_map/ppermute | solution.py:128
  93.5 2.8 %copy-start.6 = (f32[32,1152]{1,0:T(8,128)}, f32[32,1152]{1,0:T(8,128)S(1)}, u32[]{:S(2)}) copy-start(f32[32,1152]{1,0:T(8,128)S(1)} %collective-permute-done.25.refs_3_) | copy-start | bytes 442372
  96.2 0.7 copy-start.7
  96.8 0.7 copy-start.8

commit v2 on v1

--- a/solution.py
+++ b/solution.py
@@ -8,13 +8,14 @@
 from jax.experimental.pallas import tpu as pltpu
 from jax.sharding import PartitionSpec as P
 
-CHUNKS = 4
+CHUNKS = 2
 STATS_CHUNK = 1
 LANES = 128
 HI = lax.Precision.HIGHEST
 ROWS = (((1,), (1,)), ((), ()))
 WHOLE = pl.BlockSpec(memory_space=pltpu.VMEM)
-PARAMS = pltpu.CompilerParams(vmem_limit_bytes=44 << 20)
+PARAMS = pltpu.CompilerParams(vmem_limit_bytes=12 << 20)
+SMALL = pltpu.CompilerParams(vmem_limit_bytes=4 << 20)
 
 
 def eye(n):
@@ -31,22 +32,36 @@
     return aug[:, n:]
 
 
-def pass_one(all_rows, all_cols, n_cell, n_chan, chan_ref, cell_ref, slab_ref, *refs):
+def place(block, rel, n_rel, width):
+    me = lax.rem(lax.axis_index("chan"), n_rel)
+    at = (block * n_rel + lax.bitwise_xor(me, rel)) * width
+    return pl.ds(pl.multiple_of(at, width), width)
+
+
+def pass_one(all_rows, all_cols, n_cell, n_chan, chan_hbm, cell_hbm, slab_hbm, *refs):
     sends, keeps = refs[:CHUNKS], refs[CHUNKS : 2 * CHUNKS]
-    stats_ref, slab_v, sem = refs[2 * CHUNKS :]
-    core = lax.rem(lax.axis_index("chan"), 2)
-    width = slab_ref.shape[0] // (2 * CHUNKS)
+    stats_ref, slab_v, chan_ref, cell_ref, sem, small_sem = refs[2 * CHUNKS :]
+    n_rel = n_chan // 2
+    width = slab_hbm.shape[0] // (CHUNKS * n_rel)
+    chan_copy = pltpu.make_async_copy(chan_hbm, chan_ref, small_sem.at[0])
+    cell_copy = pltpu.make_async_copy(cell_hbm, cell_ref, small_sem.at[1])
+    chan_copy.start()
     jobs = []
     for k in range(CHUNKS):
-        for half, out in ((1 - core, sends[k]), (core, keeps[k])):
-            at = pl.ds(pl.multiple_of((2 * k + half) * width, width), width)
-            copy = pltpu.make_async_copy(slab_ref.at[at], slab_v.at[at], sem.at[len(jobs)])
+        for rel in [*range(1, n_rel, 2), *range(0, n_rel, 2)]:
+            at = place(k, rel, n_rel, width)
+            copy = pltpu.make_async_copy(slab_hbm.at[at], slab_v.at[at], sem.at[len(jobs)])
             copy.start()
-            jobs.append((copy, at, out))
+            if not jobs:
+                cell_copy.start()
+            out = (sends if rel % 2 else keeps)[k]
+            jobs.append((copy, at, out.at[:, pl.ds(rel // 2 * width, width)]))
+    chan_copy.wait()
     chan = chan_ref[...]
     low = chan.astype(jnp.bfloat16)
+    chan_gram = lax.dot_general(chan, chan, ROWS, precision=HI) / (all_cols * n_cell)
+    cell_copy.wait()
     cell = cell_ref[...]
-    chan_gram = lax.dot_general(chan, chan, ROWS, precision=HI) / (all_cols * n_cell)
     cell_gram = lax.dot_general(cell, cell, ROWS, precision=HI) / (all_rows * n_chan)
     total = jnp.zeros((chan.shape[0], LANES), jnp.float32)
     for copy, at, out in jobs:
@@ -76,27 +91,25 @@
     out_ref[...] = jnp.concatenate([inverse, outer, time, pad], axis=1)
 
 
-def pass_two(all_rows, all_cols, solved_ref, mttkrp_ref, slab_v, *refs):
-    own, other = refs[:CHUNKS], refs[CHUNKS : 2 * CHUNKS]
-    new_mttkrp, new_factor, out_ref = refs[2 * CHUNKS :]
+def pass_two(all_rows, all_cols, where, n_rel, solved_ref, mttkrp_ref, slab_v, *refs):
+    pieces = refs[: len(where)]
+    new_mttkrp, new_factor, out_ref = refs[len(where) :]
     n = solved_ref.shape[0]
-    core = lax.rem(lax.axis_index("chan"), 2)
-    width = slab_v.shape[0] // (2 * CHUNKS)
     cols = slab_v.shape[1]
     inverse = solved_ref[:, :n]
     time = solved_ref[:, 2 * n : 2 * n + 1] / math.sqrt(all_cols)
     total = jnp.zeros((n, cols), jnp.float32)
     gram = jnp.zeros((n, n), jnp.float32)
-    for k in range(CHUNKS):
-        for half, part in ((core, own[k]), (1 - core, other[k])):
-            at = pl.ds(pl.multiple_of((2 * k + half) * width, width), width)
-            right = mttkrp_ref[:, at] + time * part[:, :width]
-            new_mttkrp[:, at] = right
-            factor = jnp.dot(inverse, right, precision=HI)
-            new_factor[:, at] = factor
-            gram += lax.dot_general(factor, factor, ROWS, precision=HI)
-            low = factor.astype(jnp.bfloat16)
-            total += jnp.dot(low, slab_v[at], preferred_element_type=jnp.float32)
+    for (chunk, rel), piece in zip(where, pieces):
+        width = piece.shape[1]
+        at = place(chunk, rel, n_rel, width)
+        right = mttkrp_ref[:, at] + time * piece[...]
+        new_mttkrp[:, at] = right
+        factor = jnp.dot(inverse, right, precision=HI)
+        new_factor[:, at] = factor
+        gram += lax.dot_general(factor, factor, ROWS, precision=HI)
+        low = factor.astype(jnp.bfloat16)
+        total += jnp.dot(low, slab_v[at], preferred_element_type=jnp.float32)
     out_ref[:, :cols] = total
     pad = jnp.zeros((n, LANES - n), jnp.float32)
     out_ref[:, cols:] = jnp.concatenate([gram / all_rows, pad], axis=1)
@@ -134,21 +147,33 @@
     return parts[0]
 
 
-def hop(x, moves):
-    return lax.ppermute(x, "chan", [(2 * a + c, 2 * b + c) for a, b in moves for c in (0, 1)])
-
-
-def over_chips(x, n_chip):
-    chip = lax.axis_index("chan") // 2
-    far = n_chip - 1
-    half = n_chip // 2
-    for s in range(half - 1):
-        x = x + hop(x, [(s, s + 1), (far - s, far - s - 1)])
-    x = x + hop(x, [(half - 1, half), (half, half - 1)])
-    for s in reversed(range(half - 1)):
-        got = hop(x, [(s + 1, s), (far - s - 1, far - s)])
-        x = jnp.where((chip == s) | (chip == far - s), got, x)
-    return x
+def trade(x, mask, n_chan):
+    return lax.ppermute(x, "chan", [(i, i ^ mask) for i in range(n_chan)])
+
+
+def over_chan(send, keep, extra, n_chan):
+    width = keep.shape[1] // (n_chan // 4)
+    if extra is not None:
+        send = jnp.concatenate([send, extra], axis=1)
+        keep = jnp.concatenate([keep, extra], axis=1)
+    size = keep.shape[1] - (0 if extra is None else LANES)
+    mask = 1
+    while True:
+        x = keep + trade(send, mask, n_chan)
+        mask *= 2
+        if mask == n_chan // 2:
+            break
+        blocks = [x[:, i * width : (i + 1) * width] for i in range(size // width)]
+        tail = [] if extra is None else [x[:, size:]]
+        keep = jnp.concatenate(blocks[::2] + tail, axis=1) if len(blocks) > 2 or tail else blocks[0]
+        send = jnp.concatenate(blocks[1::2] + tail, axis=1) if len(blocks) > 2 or tail else blocks[1]
+        size //= 2
+    x = x + trade(x, mask, n_chan)
+    have = {0: x[:, :width]}
+    while mask > 1:
+        mask //= 2
+        have.update({rel + mask: trade(block, mask, n_chan) for rel, block in list(have.items())})
+    return have, None if extra is None else x[:, width:]
 
 
 def body(slab, cell_factor, chan_factor, cell_mttkrp, chan_mttkrp, cell_gram_acc, chan_gram_acc):
@@ -157,47 +182,55 @@
     rows, cols = slab.shape
     rank = cell_factor.shape[0]
     all_rows, all_cols = rows * n_cell, cols * n_chan
-    width = rows // (2 * CHUNKS)
+    n_rel = n_chan // 2
+    width = rows // (CHUNKS * n_rel)
     f32 = functools.partial(jax.ShapeDtypeStruct, dtype=jnp.float32)
 
     first = pl.pallas_call(
         functools.partial(pass_one, all_rows, all_cols, n_cell, n_chan),
-        in_specs=[WHOLE, WHOLE, pl.BlockSpec(memory_space=pl.ANY)],
+        in_specs=[pl.BlockSpec(memory_space=pltpu.HBM)] * 3,
         out_specs=[WHOLE] * (2 * CHUNKS + 2),
-        out_shape=[f32((rank, width))] * (2 * CHUNKS)
+        out_shape=[f32((rank, width * n_rel // 2))] * (2 * CHUNKS)
         + [f32((rank, LANES)), pltpu.VMEM((rows, cols), slab.dtype)],
-        scratch_shapes=[pltpu.SemaphoreType.DMA((2 * CHUNKS,))],
+        scratch_shapes=[
+            pltpu.VMEM(chan_factor.shape, jnp.float32),
+            pltpu.VMEM(cell_factor.shape, jnp.float32),
+            pltpu.SemaphoreType.DMA((CHUNKS * n_rel,)),
+            pltpu.SemaphoreType.DMA((2,)),
+        ],
         compiler_params=PARAMS,
         name="pass_one",
-    )(chan_factor, cell_factor, slab)
+    )(*(pltpu.with_memory_space_constraint(x, pltpu.HBM) for x in (chan_factor, cell_factor, slab)))
     sends, keeps = list(first[:CHUNKS]), list(first[CHUNKS : 2 * CHUNKS])
     stats, slab_v = first[2 * CHUNKS :]
     slab_v = pltpu.with_memory_space_constraint(slab_v, pltpu.VMEM)
 
     stats = pair_sum(over_cell(stats, n_cell))
-    sends[STATS_CHUNK] = jnp.concatenate([sends[STATS_CHUNK], stats], axis=1)
-    keeps[STATS_CHUNK] = jnp.concatenate([keeps[STATS_CHUNK], stats], axis=1)
-    swap = [(i, i ^ 1) for i in range(n_chan)]
-    own = [keep + lax.ppermute(send, "chan", swap) for send, keep in zip(sends, keeps)]
-    own = [over_chips(x, n_chan // 2) for x in own]
-    other = [lax.ppermute(x[:, :width], "chan", swap) for x in own]
+    where, pieces = [], []
+    for k in range(CHUNKS):
+        have, got = over_chan(sends[k], keeps[k], stats if k == STATS_CHUNK else None, n_chan)
+        where += [(k, rel) for rel in have]
+        pieces += have.values()
+        if got is not None:
+            summed = got
 
     row, new_cell_gram, solved = pl.pallas_call(
         solve_one,
         in_specs=[WHOLE] * 2,
         out_specs=[WHOLE] * 3,
         out_shape=[f32((1, rank)), f32((rank, rank)), f32((rank, LANES))],
+        compiler_params=SMALL,
         name="solve_one",
-    )(own[STATS_CHUNK][:, width:], cell_gram_acc)
+    )(summed, cell_gram_acc)
 
     new_cell_mttkrp, new_cell_factor, part = pl.pallas_call(
-        functools.partial(pass_two, all_rows, all_cols),
-        in_specs=[WHOLE] * (3 + 2 * CHUNKS),
+        functools.partial(pass_two, all_rows, all_cols, where, n_rel),
+        in_specs=[WHOLE] * (3 + len(where)),
         out_specs=[WHOLE] * 3,
         out_shape=[f32((rank, rows)), f32((rank, rows)), f32((rank, cols + LANES))],
         compiler_params=PARAMS,
         name="pass_two",
-    )(solved, cell_mttkrp, slab_v, *own, *other)
+    )(solved, cell_mttkrp, slab_v, *pieces)
 
     parts = over_cell(part, n_cell)
     new_chan_mttkrp, new_chan_factor, new_chan_gram = pl.pallas_call(
@@ -205,6 +238,7 @@
         in_specs=[WHOLE] * (3 + len(parts)),
         out_specs=[WHOLE] * 3,
         out_shape=[f32((rank, cols)), f32((rank, cols)), f32((rank, rank))],
+        compiler_params=SMALL,
         name="solve_two",
     )(solved, chan_mttkrp, chan_gram_acc, *parts)
     return (

time: 103 us -> 73.6 us (0.71)
  local copies, waits for them, and re-layouts: 14.1 us -> 0.06 us
  starting transfers between devices: 24.7 us -> 18.9 us
  other arithmetic: 5.57 us -> 0.17 us
  Pallas kernels: 29.1 us -> 24.4 us
  waiting for transfers between devices: 27.9 us -> 29.2 us
    unnamed x26 -> x8, local copies, waits for them, and re-layouts: 13.5 us -> 0.02 us
    ppermute x20 -> x12, starting transfers between devices: 16.8 us -> 10.8 us  [trade(): return lax.ppermute(x, 'chan', [(i, i ^ mask) for i in range(n_chan)])]
    add x12 -> x6, other arithmetic: 3.86 us -> 0.14 us  [the longest x4 0.1 us: over_chan(): x = keep + trade(send, mask, n_chan)]
    ppermute x20 -> x12, waiting for transfers between devices: 16.9 us -> 18.6 us  [trade(): return lax.ppermute(x, 'chan', [(i, i ^ mask) for i in range(n_chan)])]
    pallas_call x1, Pallas kernels: 6.72 us -> 5.13 us  [body(): pl.pallas_call(functools.partial(pass_two, all_rows, all_cols, where, n_r...]
    pallas_call x1, Pallas kernels: 7.08 us -> 5.74 us  [body(): pl.pallas_call(solve_one, in_specs=[WHOLE] * 2, out_specs=[WHOLE] * 3, ou...]
    pallas_call x1, Pallas kernels: 4.96 us -> 3.73 us  [body(): pl.pallas_call(functools.partial(solve_two, all_rows, len(parts)), in_spe...]
  transfers between devices with their start and end apart: 26 -> 18, of which waited for: 13 -> 11; matrix products, arithmetic and copies ran while one was open for 4% -> 0% of each run, Pallas kernels for 7% -> 8%
where the time goes in v2:
time: 73.6 us; the launch traced here: 73.5 us
  waiting for transfers between devices  29.2 us (40%)
  Pallas kernels  24.4 us (33%)
  starting transfers between devices  18.9 us (26%)
  between operations  0.8 us (1%)
    ppermute x12, waiting for transfers between devices, trade(): return lax.ppermute(x, 'chan', [(i, i ^ mask) for i in range(n_chan)])  18.6 us
    ppermute x12, starting transfers between devices, trade(): return lax.ppermute(x, 'chan', [(i, i ^ mask) for i in range(n_chan)])  10.8 us
    ppermute x6, waiting for transfers between devices, over_cell(): lax.ppermute(x, 'cell', [(i, i ^ m) for i in range(n_cell)])  10.5 us
    pallas_call x1, Pallas kernels, body(): pl.pallas_call(functools.partial(pass_one, all_rows, all_cols, n_cell, n_...  9.75 us
    ppermute x6, starting transfers between devices, over_cell(): lax.ppermute(x, 'cell', [(i, i ^ m) for i in range(n_cell)])  8.09 us
    pallas_call x1, Pallas kernels, body(): pl.pallas_call(solve_one, in_specs=[WHOLE] * 2, out_specs=[WHOLE] * 3, ou...  5.74 us
    pallas_call x1, Pallas kernels, body(): pl.pallas_call(functools.partial(pass_two, all_rows, all_cols, where, n_r...  5.13 us
    pallas_call x1, Pallas kernels, body(): pl.pallas_call(functools.partial(solve_two, all_rows, len(parts)), in_spe...  3.73 us
  transfers between devices with their start and end apart: 18, of which 11 were waited for; matrix products, arithmetic and copies ran while one was open for 0% of the time, Pallas kernels for 8%

profile of v2, /device:TPU:0, one launch (start us, length us, event | category | flops | bytes accessed | tf_op | source)
XLA Modules:
  0.0 73.5 jit_solution(9285376309043572871)
XLA Ops:
  0.6 0.0 copy-start.3
  0.6 0.0 copy-start
  0.7 0.0 copy-start.2
  0.7 0.0 copy-start.1
  0.7 9.8 %pass_one.1 = (f32[32,2048]{1,0:T(8,128)S(1)}, f32[32,2048]{1,0:T(8,128)S(1)}, f32[32,2048]{1,0:T(8,128)S(1)}, f32[32,2048]{1,0:T(8,128)S(1)}, f32[32,128]{1,0:T(8,128)S(1)}, /*index=5*/bf16[8192,1024]{1,0:T(8,128)(2,1)S(1)}) custom-call(f32[32,1024]{1,0:T(8,128)} %chan_hbm.1, f32[32,8192]{1,0:T(8,128)} %cell_hbm.1, bf16[8192,1024]{1,0:T(8,128)(2,1)} %slab_hbm.1), custom_call_target="tpu_custom_call" | custom-call | tf_op jit(solution)/shard_map/pass_one/pallas_call | solution.py:189
  10.4 4.0 %collective-permute-start.2 = (f32[32,128]{1,0:T(8,128)S(1)}, f32[32,128]{1,0:T(8,128)S(1)}, u32[]{:S(2)}, u32[]{:S(2)}) collective-permute-start(f32[32,128]{1,0:T(8,128)S(1)} %get-tuple-element.23), channel_id=1, source_target_pairs={{0,24},{8,16},{16,8},{24,0},{1,25},{9,17},{17,9},{25,1},{2,26},{10... | collective-permute-start | bytes 49160 | tf_op jit(solution)/shard_map/ppermute | solution.py:141
  14.4 0.5 collective-permute-start.1
  14.9 0.1 collective-permute-start
  15.0 1.1 %collective-permute-done.2 = f32[32,128]{1,0:T(8,128)S(1)} collective-permute-done((f32[32,128]{1,0:T(8,128)S(1)}, f32[32,128]{1,0:T(8,128)S(1)}, u32[]{:S(2)}, u32[]{:S(2)}) %collective-permute-start.2) | collective-permute-done | bytes 16416 | tf_op jit(solution)/shard_map/ppermute | solution.py:141
  16.1 2.0 %collective-permute-done.1 = f32[32,128]{1,0:T(8,128)S(1)} collective-permute-done((f32[32,128]{1,0:T(8,128)S(1)}, f32[32,128]{1,0:T(8,128)S(1)}, u32[]{:S(2)}, u32[]{:S(2)}) %collective-permute-start.1) | collective-permute-done | bytes 16416 | tf_op jit(solution)/shard_map/ppermute | solution.py:141
  18.1 0.5 collective-permute-done
  18.7 0.1 collective-permute-start.3
  18.8 0.5 collective-permute-start.6
  19.3 1.0 %collective-permute-done.3 = f32[32,2176]{1,0:T(8,128)S(1)} collective-permute-done((f32[32,2176]{1,0:T(8,128)S(1)}, f32[32,2176]{1,0:T(8,128)S(1)}, u32[]{:S(2)}, u32[]{:S(2)}) %collective-permute-start.3) | collective-permute-done | bytes 278560 | tf_op jit(solution)/shard_map/ppermute | solution.py:151
  20.4 1.6 %collective-permute-start.4 = (f32[32,1152]{1,0:T(8,128)S(1)}, f32[32,1152]{1,0:T(8,128)S(1)}, u32[]{:S(2)}, u32[]{:S(2)}) collective-permute-start(f32[32,1152]{1,0:T(8,128)S(1)} %concatenate.16), channel_id=1, source_target_pairs={{0,2},{1,3},{2,0},{3,1},{4,6},{5,7},{6,4},{7,5},{8,10},{9,11},{10,... | collective-permute-start | bytes 442376 | tf_op jit(solution)/shard_map/ppermute | solution.py:151
  22.0 0.0 collective-permute-done.6
  22.0 0.5 collective-permute-start.7
  22.6 4.5 %collective-permute-done.4 = f32[32,1152]{1,0:T(8,128)S(1)} collective-permute-done((f32[32,1152]{1,0:T(8,128)S(1)}, f32[32,1152]{1,0:T(8,128)S(1)}, u32[]{:S(2)}, u32[]{:S(2)}) %collective-permute-start.4) | collective-permute-done | bytes 147488 | tf_op jit(solution)/shard_map/ppermute | solution.py:151
  27.1 2.7 %collective-permute-start.5 = (f32[32,1152]{1,0:T(8,128)S(1)}, f32[32,1152]{1,0:T(8,128)S(1)}, u32[]{:S(2)}, u32[]{:S(2)}) collective-permute-start(f32[32,1152]{1,0:T(8,128)S(1)} %maximum_add_fusion), channel_id=1, source_target_pairs={{0,4},{1,5},{2,6},{3,7},{4,0},{5,1},{6,2},{7,3},{8,12},{9,13},{10,... | collective-permute-start | bytes 442376 | tf_op jit(solution)/shard_map/ppermute | solution.py:151
  29.8 0.0 collective-permute-done.7
  29.8 2.8 %collective-permute-start.8 = (f32[32,1024]{1,0:T(8,128)S(1)}, f32[32,1024]{1,0:T(8,128)S(1)}, u32[]{:S(2)}, u32[]{:S(2)}) collective-permute-start(f32[32,1024]{1,0:T(8,128)S(1)} %slice_add_fusion), channel_id=1, source_target_pairs={{0,4},{1,5},{2,6},{3,7},{4,0},{5,1},{6,2},{7,3},{8,12},{9,13},{10,... | collective-permute-start | bytes 393224 | tf_op jit(solution)/shard_map/ppermute | solution.py:151
  32.6 8.8 %collective-permute-done.8 = f32[32,1024]{1,0:T(8,128)S(1)} collective-permute-done((f32[32,1024]{1,0:T(8,128)S(1)}, f32[32,1024]{1,0:T(8,128)S(1)}, u32[]{:S(2)}, u32[]{:S(2)}) %collective-permute-start.8) | collective-permute-done | bytes 131104 | tf_op jit(solution)/shard_map/ppermute | solution.py:151
  41.4 0.5 collective-permute-start.9
  41.9 0.0 collective-permute-done.5
  41.9 1.6 %collective-permute-start.12 = (f32[32,1024]{1,0:T(8,128)S(1)}, f32[32,1024]{1,0:T(8,128)S(1)}, u32[]{:S(2)}, u32[]{:S(2)}) collective-permute-start(f32[32,1024]{1,0:T(8,128)S(1)} %slice.31.refs_4_), channel_id=1, source_target_pairs={{0,2},{1,3},{2,0},{3,1},{4,6},{5,7},{6,4},{7,5},{8,10},{9,11},{10,... | collective-permute-start | bytes 393224 | tf_op jit(solution)/shard_map/ppermute | solution.py:151
  43.6 0.0 collective-permute-start.10
  43.6 0.5 collective-permute-start.13
  44.1 2.9 %collective-permute-done.9.refs_1_ = f32[32,1024]{1,0:T(8,128)S(1)} collective-permute-done((f32[32,1024]{1,0:T(8,128)S(1)}, f32[32,1024]{1,0:T(8,128)S(1)}, u32[]{:S(2)}, u32[]{:S(2)}) %collective-permute-start.9) | collective-permute-done | bytes 131104 | tf_op jit(solution)/shard_map/ppermute | solution.py:151
  47.0 0.0 collective-permute-start.11
  47.0 1.4 %collective-permute-done.12.refs_5_ = f32[32,1024]{1,0:T(8,128)S(1)} collective-permute-done((f32[32,1024]{1,0:T(8,128)S(1)}, f32[32,1024]{1,0:T(8,128)S(1)}, u32[]{:S(2)}, u32[]{:S(2)}) %collective-permute-start.12) | collective-permute-done | bytes 131104 | tf_op jit(solution)/shard_map/ppermute | solution.py:151
  48.4 0.0 collective-permute-start.14
  48.4 0.0 copy-done.3
  48.4 5.7 %solve_one.1 = (f32[1,32]{1,0:T(1,128)}, f32[32,32]{1,0:T(8,128)}, f32[32,128]{1,0:T(8,128)S(1)}) custom-call(f32[32,128]{1,0:T(8,128)S(1)} %slice.28.stats_ref, f32[32,32]{1,0:T(8,128)S(1)} %copy-done.3), custom_call_target="tpu_custom_call" | custom-call | tf_op jit(solution)/shard_map/solve_one/pallas_call | solution.py:217
  54.1 0.0 collective-permute-done.10.refs_2_
  54.2 0.0 collective-permute-done.13.refs_6_
  54.2 0.0 collective-permute-done.11.refs_3_
  54.2 0.0 collective-permute-done.14.refs_7_
  54.2 0.0 copy-done
  54.2 5.1 %pass_two.1 = (f32[32,8192]{1,0:T(8,128)}, f32[32,8192]{1,0:T(8,128)}, f32[32,1152]{1,0:T(8,128)S(1)}) custom-call(f32[32,128]{1,0:T(8,128)S(1)} %get-tuple-element.26.solved_ref, f32[32,8192]{1,0:T(8,128)S(1)} %copy-done, bf16[8192,1024]{1,0:T(8,128)(2,1)S(1)} %get-tuple-element.27.slab_v, f32[32,1024]{1,0:T(8,128)S(1)} %add.35.refs_0_, ...), custom_call_target="tpu_custom_call" | custom-call | tf_op jit(solution)/shard_map/pass_two/pallas_call | solution.py:226
  59.3 1.5 %collective-permute-start.17 = (f32[32,1152]{1,0:T(8,128)S(1)}, f32[32,1152]{1,0:T(8,128)S(1)}, u32[]{:S(2)}, u32[]{:S(2)}) collective-permute-start(f32[32,1152]{1,0:T(8,128)S(1)} %get-tuple-element.31.refs_0_), channel_id=1, source_target_pairs={{0,24},{8,16},{16,8},{24,0},{1,25},{9,17},{17,9},{25,1},{2,26},{10... | collective-permute-start | bytes 442376 | tf_op jit(solution)/shard_map/ppermute | solution.py:141
  60.8 0.5 collective-permute-start.16
  61.3 1.5 %collective-permute-start.15 = (f32[32,1152]{1,0:T(8,128)S(1)}, f32[32,1152]{1,0:T(8,128)S(1)}, u32[]{:S(2)}, u32[]{:S(2)}) collective-permute-start(f32[32,1152]{1,0:T(8,128)S(1)} %get-tuple-element.31.refs_0_), channel_id=1, source_target_pairs={{0,8},{8,0},{16,24},{24,16},{1,9},{9,1},{17,25},{25,17},{2,10},{10... | collective-permute-start | bytes 442376 | tf_op jit(solution)/shard_map/ppermute | solution.py:141
  62.8 4.1 %collective-permute-done.17.refs_3_ = f32[32,1152]{1,0:T(8,128)S(1)} collective-permute-done((f32[32,1152]{1,0:T(8,128)S(1)}, f32[32,1152]{1,0:T(8,128)S(1)}, u32[]{:S(2)}, u32[]{:S(2)}) %collective-permute-start.17) | collective-permute-done | bytes 147488 | tf_op jit(solution)/shard_map/ppermute | solution.py:141
  66.9 2.7 %collective-permute-done.16.refs_2_ = f32[32,1152]{1,0:T(8,128)S(1)} collective-permute-done((f32[32,1152]{1,0:T(8,128)S(1)}, f32[32,1152]{1,0:T(8,128)S(1)}, u32[]{:S(2)}, u32[]{:S(2)}) %collective-permute-start.16) | collective-permute-done | bytes 147488 | tf_op jit(solution)/shard_map/ppermute | solution.py:141
  69.6 0.1 collective-permute-done.15.refs_1_
  69.7 0.0 copy-done.2
  69.7 0.0 copy-done.1
  69.8 3.7 %solve_two.1 = (f32[32,1024]{1,0:T(8,128)}, f32[32,1024]{1,0:T(8,128)}, f32[32,32]{1,0:T(8,128)}) custom-call(f32[32,128]{1,0:T(8,128)S(1)} %get-tuple-element.26.solved_ref, f32[32,1024]{1,0:T(8,128)S(1)} %copy-done.1, f32[32,32]{1,0:T(8,128)S(1)} %copy-done.2, f32[32,1152]{1,0:T(8,128)S(1)} %get-tuple-element.31.refs_0_, ...), custom_call_target="tpu_custom_call" | custom-call | tf_op jit(solution)/shard_map/solve_two/pallas_call | solution.py:236
  (14 shorter events, 0.2 us)
Async XLA Ops:
  0.6 47.8 %copy-start.3 = (f32[32,32]{1,0:T(8,128)S(1)}, f32[32,32]{1,0:T(8,128)}, u32[]{:S(2)}) copy-start(f32[32,32]{1,0:T(8,128)} %acc_ref.2) | copy-start | bytes 12292
  0.6 53.5 %copy-start = (f32[32,8192]{1,0:T(8,128)S(1)}, f32[32,8192]{1,0:T(8,128)}, u32[]{:S(2)}) copy-start(f32[32,8192]{1,0:T(8,128)} %mttkrp_ref.2) | copy-start | bytes 3145732
  0.7 69.1 %copy-start.2 = (f32[32,32]{1,0:T(8,128)S(1)}, f32[32,32]{1,0:T(8,128)}, u32[]{:S(2)}) copy-start(f32[32,32]{1,0:T(8,128)} %acc_ref.3) | copy-start | bytes 12292
  0.7 69.1 %copy-start.1 = (f32[32,1024]{1,0:T(8,128)S(1)}, f32[32,1024]{1,0:T(8,128)}, u32[]{:S(2)}) copy-start(f32[32,1024]{1,0:T(8,128)} %mttkrp_ref.3) | copy-start | bytes 393220
  10.4 5.7 %collective-permute-start.2 = (f32[32,128]{1,0:T(8,128)S(1)}, f32[32,128]{1,0:T(8,128)S(1)}, u32[]{:S(2)}, u32[]{:S(2)}) collective-permute-start(f32[32,128]{1,0:T(8,128)S(1)} %get-tuple-element.23), channel_id=1, source_target_pairs={{0,24},{8,16},{16,8},{24,0},{1,25},{9,17},{17,9},{25,1},{2,26},{10... | collective-permute-start | bytes 49160 | tf_op jit(solution)/shard_map/ppermute | solution.py:141
  14.4 3.7 %collective-permute-start.1 = (f32[32,128]{1,0:T(8,128)S(1)}, f32[32,128]{1,0:T(8,128)S(1)}, u32[]{:S(2)}, u32[]{:S(2)}) collective-permute-start(f32[32,128]{1,0:T(8,128)S(1)} %get-tuple-element.23), channel_id=1, source_target_pairs={{0,16},{8,24},{16,0},{24,8},{1,17},{9,25},{17,1},{25,9},{2,18},{10... | collective-permute-start | bytes 49160 | tf_op jit(solution)/shard_map/ppermute | solution.py:141
  14.9 3.7 %collective-permute-start = (f32[32,128]{1,0:T(8,128)S(1)}, f32[32,128]{1,0:T(8,128)S(1)}, u32[]{:S(2)}, u32[]{:S(2)}) collective-permute-start(f32[32,128]{1,0:T(8,128)S(1)} %get-tuple-element.23), channel_id=1, source_target_pairs={{0,8},{8,0},{16,24},{24,16},{1,9},{9,1},{17,25},{25,17},{2,10},{10... | collective-permute-start | bytes 49160 | tf_op jit(solution)/shard_map/ppermute | solution.py:141
  18.7 1.6 %collective-permute-start.3 = (f32[32,2176]{1,0:T(8,128)S(1)}, f32[32,2176]{1,0:T(8,128)S(1)}, u32[]{:S(2)}, u32[]{:S(2)}) collective-permute-start(f32[32,2176]{1,0:T(8,128)S(1)} %pad_maximum_fusion), channel_id=1, source_target_pairs={{0,1},{1,0},{2,3},{3,2},{4,5},{5,4},{6,7},{7,6},{8,9},{9,8},{10,11... | collective-permute-start | bytes 835592 | tf_op jit(solution)/shard_map/ppermute | solution.py:151
  18.8 3.2 %collective-permute-start.6 = (f32[32,2048]{1,0:T(8,128)S(1)}, f32[32,2048]{1,0:T(8,128)S(1)}, u32[]{:S(2)}, u32[]{:S(2)}) collective-permute-start(f32[32,2048]{1,0:T(8,128)S(1)} %get-tuple-element.29), channel_id=1, source_target_pairs={{0,1},{1,0},{2,3},{3,2},{4,5},{5,4},{6,7},{7,6},{8,9},{9,8},{10,11... | collective-permute-start | bytes 786440 | tf_op jit(solution)/shard_map/ppermute | solution.py:151
  20.4 6.8 %collective-permute-start.4 = (f32[32,1152]{1,0:T(8,128)S(1)}, f32[32,1152]{1,0:T(8,128)S(1)}, u32[]{:S(2)}, u32[]{:S(2)}) collective-permute-start(f32[32,1152]{1,0:T(8,128)S(1)} %concatenate.16), channel_id=1, source_target_pairs={{0,2},{1,3},{2,0},{3,1},{4,6},{5,7},{6,4},{7,5},{8,10},{9,11},{10,... | collective-permute-start | bytes 442376 | tf_op jit(solution)/shard_map/ppermute | solution.py:151
  22.0 7.7 %collective-permute-start.7 = (f32[32,1024]{1,0:T(8,128)S(1)}, f32[32,1024]{1,0:T(8,128)S(1)}, u32[]{:S(2)}, u32[]{:S(2)}) collective-permute-start(f32[32,1024]{1,0:T(8,128)S(1)} %slice.30), channel_id=1, source_target_pairs={{0,2},{1,3},{2,0},{3,1},{4,6},{5,7},{6,4},{7,5},{8,10},{9,11},{10,... | collective-permute-start | bytes 393224 | tf_op jit(solution)/shard_map/ppermute | solution.py:151
  27.1 14.8 %collective-permute-start.5 = (f32[32,1152]{1,0:T(8,128)S(1)}, f32[32,1152]{1,0:T(8,128)S(1)}, u32[]{:S(2)}, u32[]{:S(2)}) collective-permute-start(f32[32,1152]{1,0:T(8,128)S(1)} %maximum_add_fusion), channel_id=1, source_target_pairs={{0,4},{1,5},{2,6},{3,7},{4,0},{5,1},{6,2},{7,3},{8,12},{9,13},{10,... | collective-permute-start | bytes 442376 | tf_op jit(solution)/shard_map/ppermute | solution.py:151
  29.8 11.5 %collective-permute-start.8 = (f32[32,1024]{1,0:T(8,128)S(1)}, f32[32,1024]{1,0:T(8,128)S(1)}, u32[]{:S(2)}, u32[]{:S(2)}) collective-permute-start(f32[32,1024]{1,0:T(8,128)S(1)} %slice_add_fusion), channel_id=1, source_target_pairs={{0,4},{1,5},{2,6},{3,7},{4,0},{5,1},{6,2},{7,3},{8,12},{9,13},{10,... | collective-permute-start | bytes 393224 | tf_op jit(solution)/shard_map/ppermute | solution.py:151
  41.4 5.6 %collective-permute-start.9 = (f32[32,1024]{1,0:T(8,128)S(1)}, f32[32,1024]{1,0:T(8,128)S(1)}, u32[]{:S(2)}, u32[]{:S(2)}) collective-permute-start(f32[32,1024]{1,0:T(8,128)S(1)} %add.35.refs_0_), channel_id=1, source_target_pairs={{0,2},{1,3},{2,0},{3,1},{4,6},{5,7},{6,4},{7,5},{8,10},{9,11},{10,... | collective-permute-start | bytes 393224 | tf_op jit(solution)/shard_map/ppermute | solution.py:151
  41.9 6.4 %collective-permute-start.12 = (f32[32,1024]{1,0:T(8,128)S(1)}, f32[32,1024]{1,0:T(8,128)S(1)}, u32[]{:S(2)}, u32[]{:S(2)}) collective-permute-start(f32[32,1024]{1,0:T(8,128)S(1)} %slice.31.refs_4_), channel_id=1, source_target_pairs={{0,2},{1,3},{2,0},{3,1},{4,6},{5,7},{6,4},{7,5},{8,10},{9,11},{10,... | collective-permute-start | bytes 393224 | tf_op jit(solution)/shard_map/ppermute | solution.py:151
  43.6 10.6 %collective-permute-start.10 = (f32[32,1024]{1,0:T(8,128)S(1)}, f32[32,1024]{1,0:T(8,128)S(1)}, u32[]{:S(2)}, u32[]{:S(2)}) collective-permute-start(f32[32,1024]{1,0:T(8,128)S(1)} %add.35.refs_0_), channel_id=1, source_target_pairs={{0,1},{1,0},{2,3},{3,2},{4,5},{5,4},{6,7},{7,6},{8,9},{9,8},{10,11... | collective-permute-start | bytes 393224 | tf_op jit(solution)/shard_map/ppermute | solution.py:151
  43.6 10.6 %collective-permute-start.13 = (f32[32,1024]{1,0:T(8,128)S(1)}, f32[32,1024]{1,0:T(8,128)S(1)}, u32[]{:S(2)}, u32[]{:S(2)}) collective-permute-start(f32[32,1024]{1,0:T(8,128)S(1)} %slice.31.refs_4_), channel_id=1, source_target_pairs={{0,1},{1,0},{2,3},{3,2},{4,5},{5,4},{6,7},{7,6},{8,9},{9,8},{10,11... | collective-permute-start | bytes 393224 | tf_op jit(solution)/shard_map/ppermute | solution.py:151
  47.0 7.2 %collective-permute-start.11 = (f32[32,1024]{1,0:T(8,128)S(1)}, f32[32,1024]{1,0:T(8,128)S(1)}, u32[]{:S(2)}, u32[]{:S(2)}) collective-permute-start(f32[32,1024]{1,0:T(8,128)S(1)} %collective-permute-done.9.refs_1_), channel_id=1, source_target_pairs={{0,1},{1,0},{2,3},{3,2},{4,5},{5,4},{6,7},{7,6},{8,9},{9,8},{10,11... | collective-permute-start | bytes 393224 | tf_op jit(solution)/shard_map/ppermute | solution.py:151
  48.4 5.8 %collective-permute-start.14 = (f32[32,1024]{1,0:T(8,128)S(1)}, f32[32,1024]{1,0:T(8,128)S(1)}, u32[]{:S(2)}, u32[]{:S(2)}) collective-permute-start(f32[32,1024]{1,0:T(8,128)S(1)} %collective-permute-done.12.refs_5_), channel_id=1, source_target_pairs={{0,1},{1,0},{2,3},{3,2},{4,5},{5,4},{6,7},{7,6},{8,9},{9,8},{10,11... | collective-permute-start | bytes 393224 | tf_op jit(solution)/shard_map/ppermute | solution.py:151
  59.3 7.6 %collective-permute-start.17 = (f32[32,1152]{1,0:T(8,128)S(1)}, f32[32,1152]{1,0:T(8,128)S(1)}, u32[]{:S(2)}, u32[]{:S(2)}) collective-permute-start(f32[32,1152]{1,0:T(8,128)S(1)} %get-tuple-element.31.refs_0_), channel_id=1, source_target_pairs={{0,24},{8,16},{16,8},{24,0},{1,25},{9,17},{17,9},{25,1},{2,26},{10... | collective-permute-start | bytes 442376 | tf_op jit(solution)/shard_map/ppermute | solution.py:141
  60.8 8.8 %collective-permute-start.16 = (f32[32,1152]{1,0:T(8,128)S(1)}, f32[32,1152]{1,0:T(8,128)S(1)}, u32[]{:S(2)}, u32[]{:S(2)}) collective-permute-start(f32[32,1152]{1,0:T(8,128)S(1)} %get-tuple-element.31.refs_0_), channel_id=1, source_target_pairs={{0,16},{8,24},{16,0},{24,8},{1,17},{9,25},{17,1},{25,9},{2,18},{10... | collective-permute-start | bytes 442376 | tf_op jit(solution)/shard_map/ppermute | solution.py:141
  61.3 8.4 %collective-permute-start.15 = (f32[32,1152]{1,0:T(8,128)S(1)}, f32[32,1152]{1,0:T(8,128)S(1)}, u32[]{:S(2)}, u32[]{:S(2)}) collective-permute-start(f32[32,1152]{1,0:T(8,128)S(1)} %get-tuple-element.31.refs_0_), channel_id=1, source_target_pairs={{0,8},{8,0},{16,24},{24,16},{1,9},{9,1},{17,25},{25,17},{2,10},{10... | collective-permute-start | bytes 442376 | tf_op jit(solution)/shard_map/ppermute | solution.py:141

commit v3 on v2

v3 whole, which is shorter than its diff:
```python
import functools
import math

import jax
import jax.numpy as jnp
from jax import lax
from jax.experimental import pallas as pl
from jax.experimental.pallas import tpu as pltpu
from jax.sharding import PartitionSpec as P

CHUNKS = 2
LANES = 128
HI = lax.Precision.HIGHEST
ROWS = (((1,), (1,)), ((), ()))
WHOLE = pl.BlockSpec(memory_space=pltpu.VMEM)
PARAMS = pltpu.CompilerParams(vmem_limit_bytes=12 << 20)


def cost(us):
    return pl.CostEstimate(flops=int(us * 1e9), bytes_accessed=int(us * 3e6), transcendentals=0)


SMALL = pltpu.CompilerParams(vmem_limit_bytes=4 << 20)


def eye(n):
    i = lax.broadcasted_iota(jnp.int32, (n, n), 0)
    j = lax.broadcasted_iota(jnp.int32, (n, n), 1)
    return (i == j).astype(jnp.float32)


def eliminate(aug, n):
    rows = lax.broadcasted_iota(jnp.int32, aug.shape, 0)
    for k in range(n):
        row = aug[k : k + 1, :] * (1.0 / aug[k : k + 1, k : k + 1])
        aug = jnp.where(rows == k, row, aug - aug[:, k : k + 1] * row)
    return aug[:, n:]


def place(rel, n_rel, width):
    me = lax.rem(lax.axis_index("chan"), n_rel)
    return pl.multiple_of(lax.bitwise_xor(me, rel) * width, width)


def multiply(start, n_rel, low_ref, cell_ref, slab_hbm, slab_v, sem, send_ref, keep_ref, load):
    width = slab_v.shape[0] // n_rel
    jobs = []
    for rel in [*range(1, n_rel, 2), *range(0, n_rel, 2)]:
        at = place(rel, n_rel, width)
        rows = pl.ds(pl.multiple_of(start + at, width), width)
        here = pl.ds(at, width)
        copy = pltpu.make_async_copy(slab_hbm.at[rows], slab_v.at[here], sem.at[len(jobs)])
        copy.start()
        out = (send_ref if rel % 2 else keep_ref).at[:, pl.ds(rel // 2 * width, width)]
        jobs.append((copy, rows, here, out))
    load()
    low = low_ref[...].astype(jnp.bfloat16)
    total = jnp.zeros((low.shape[0], LANES), jnp.float32)
    for copy, rows, here, out in jobs:
        copy.wait()
        part = lax.dot_general(low, slab_v[here], ROWS, preferred_element_type=jnp.float32)
        out[...] = part
        part = part * cell_ref[:, rows]
        for j in range(0, width, LANES):
            total += part[:, j : j + LANES]
    return total


def copies(pairs, sem):
    moves = [pltpu.make_async_copy(a, b, sem.at[i]) for i, (a, b) in enumerate(pairs)]
    for move in moves:
        move.start()
    return lambda: [move.wait() for move in moves]


def pass_one_a(n_rel, chan_hbm, cell_hbm, slab_hbm, send_ref, keep_ref, rhs_ref, slab_v, chan_ref, cell_ref, sem, small_sem):
    load = copies([(chan_hbm, chan_ref), (cell_hbm, cell_ref)], small_sem)
    rhs_ref[...] = multiply(0, n_rel, chan_ref, cell_ref, slab_hbm, slab_v, sem, send_ref, keep_ref, load)


def pass_one_b(
    start, all_rows, all_cols, n_cell, n_chan, chan_hbm, cell_hbm, slab_hbm, rhs_in_ref, after_hbm,
    send_ref, keep_ref, stats_ref, slab_v, chan_ref, cell_ref, sem, small_sem,
):
    del after_hbm
    n_rel = n_chan // 2
    load = copies([(chan_hbm, chan_ref), (cell_hbm, cell_ref)], small_sem)
    total = multiply(start, n_rel, chan_ref, cell_ref, slab_hbm, slab_v, sem, send_ref, keep_ref, load)
    chan, cell = chan_ref[...], cell_ref[...]
    chan_gram = lax.dot_general(chan, chan, ROWS, precision=HI) / (all_cols * n_cell)
    cell_gram = lax.dot_general(cell, cell, ROWS, precision=HI) / (all_rows * n_chan)
    total = total + rhs_in_ref[...]
    rhs = jnp.sum(total, axis=1, keepdims=True) / math.sqrt(all_rows * all_cols)
    pad = jnp.zeros((chan.shape[0], LANES - 1 - 2 * chan.shape[0]), jnp.float32)
    stats_ref[...] = jnp.concatenate([cell_gram, chan_gram, rhs, pad], axis=1)


def solve_one(stats_ref, acc_ref, row_ref, gram_ref, out_ref):
    stats = stats_ref[...]
    n = stats.shape[0]
    cell_norm, chan_norm, rhs = stats[:, :n], stats[:, n : 2 * n], stats[:, 2 * n : 2 * n + 1]
    time = eliminate(jnp.concatenate([cell_norm * chan_norm, rhs], axis=1), n)
    row = jnp.sum(eye(n) * time, axis=0, keepdims=True)
    outer = time * row
    gram = acc_ref[...] + chan_norm * outer
    inverse = eliminate(jnp.concatenate([gram, eye(n)], axis=1), n)
    row_ref[...] = row
    gram_ref[...] = gram
    pad = jnp.zeros((n, LANES - 2 * n - 1), jnp.float32)
    out_ref[...] = jnp.concatenate([inverse, outer, time, pad], axis=1)


def pass_two(all_rows, all_cols, where, n_rel, resume, solved_ref, mttkrp_ref, *refs):
    slabs, refs = refs[:CHUNKS], refs[CHUNKS:]
    pieces, refs = refs[: len(where)], refs[len(where) :]
    before, refs = (refs[:3], refs[3:]) if resume else (None, refs)
    mttkrp_hbm, factor_hbm, out_ref, mttkrp_v, factor_v, sem = refs
    n = solved_ref.shape[0]
    cols = slabs[0].shape[1]
    inverse = solved_ref[:, :n]
    time = solved_ref[:, 2 * n : 2 * n + 1] / math.sqrt(all_cols)
    total = before[2][:, :cols] if resume else jnp.zeros((n, cols), jnp.float32)
    gram = before[2][:, cols : cols + n] if resume else jnp.zeros((n, n), jnp.float32)
    moves = []
    for i, ((chunk, rel), piece) in enumerate(zip(where, pieces)):
        width = piece.shape[1]
        at = place(rel, n_rel, width)
        rows = pl.ds(pl.multiple_of(chunk * n_rel * width + at, width), width)
        right = mttkrp_ref[:, rows] + time * piece[...]
        mttkrp_v[i] = right
        factor = jnp.dot(inverse, right, precision=HI)
        factor_v[i] = factor
        for a, b in ((mttkrp_v, mttkrp_hbm), (factor_v, factor_hbm)):
            moves.append(pltpu.make_async_copy(a.at[i], b.at[:, rows], sem.at[len(moves)]))
            moves[-1].start()
        gram += lax.dot_general(factor, factor, ROWS, precision=HI) / all_rows
        low = factor.astype(jnp.bfloat16)
        total += jnp.dot(low, slabs[chunk][pl.ds(at, width)], preferred_element_type=jnp.float32)
    out_ref[:, :cols] = total
    out_ref[:, cols:] = jnp.concatenate([gram, jnp.zeros((n, LANES - n), jnp.float32)], axis=1)
    for move in moves:
        move.wait()


def solve_two(all_rows, n_parts, solved_ref, mttkrp_ref, acc_ref, *refs):
    parts = [r[...] for r in refs[:n_parts]]
    new_mttkrp, new_factor, new_gram = refs[n_parts:]
    while len(parts) > 1:
        parts = [a + b for a, b in zip(parts[::2], parts[1::2])]
    (summed,) = parts
    n, cols = mttkrp_ref.shape
    outer = solved_ref[:, n : 2 * n]
    time = solved_ref[:, 2 * n : 2 * n + 1] / math.sqrt(all_rows)
    gram = acc_ref[...] + summed[:, cols : cols + n] * outer
    inverse = eliminate(jnp.concatenate([gram, eye(n)], axis=1), n)
    right = mttkrp_ref[...] + time * summed[:, :cols]
    new_mttkrp[...] = right
    new_factor[...] = jnp.dot(inverse, right, precision=HI)
    new_gram[...] = gram


def over_cell(x, n_cell):
    masks = 1
    while masks < n_cell // 4:
        masks *= 2
        x = x + lax.ppermute(x, "cell", [(i, i ^ (2 * masks)) for i in range(n_cell)])
    near = [m for m in (1, 2, 3) if m < n_cell]
    return [x] + [lax.ppermute(x, "cell", [(i, i ^ m) for i in range(n_cell)]) for m in near]


def pair_sum(parts):
    while len(parts) > 1:
        parts = [a + b for a, b in zip(parts[::2], parts[1::2])]
    return parts[0]


def trade(x, mask, n_chan):
    return lax.ppermute(x, "chan", [(i, i ^ mask) for i in range(n_chan)])


def over_chan(x, n_chan):
    width = x.shape[1] // (n_chan // 4)
    mask = 2
    while mask < n_chan // 2:
        blocks = [x[:, i : i + width] for i in range(0, x.shape[1], width)]
        keep, send = (jnp.concatenate(b, axis=1) if len(b) > 1 else b[0] for b in (blocks[::2], blocks[1::2]))
        x = keep + trade(send, mask, n_chan)
        mask *= 2
    have = {0: x + trade(x, mask, n_chan)}
    while mask > 2:
        mask //= 2
        have.update({rel + mask: trade(block, mask, n_chan) for rel, block in list(have.items())})
    have.update({rel + 1: trade(block, 1, n_chan) for rel, block in list(have.items())})
    return have


def body(slab, cell_factor, chan_factor, cell_mttkrp, chan_mttkrp, cell_gram_acc, chan_gram_acc):
    n_cell = lax.axis_size("cell")
    n_chan = lax.axis_size("chan")
    rows, cols = slab.shape
    rank = cell_factor.shape[0]
    all_rows, all_cols = rows * n_cell, cols * n_chan
    n_rel = n_chan // 2
    start = rows // CHUNKS
    width = start // n_rel
    f32 = functools.partial(jax.ShapeDtypeStruct, dtype=jnp.float32)
    hbm = pl.BlockSpec(memory_space=pltpu.HBM)
    inputs = [pltpu.with_memory_space_constraint(x, pltpu.HBM) for x in (chan_factor, cell_factor, slab)]
    half = f32((rank, start // 2))
    tile = f32((rank, LANES))
    slab_half = pltpu.VMEM((start, cols), slab.dtype)
    scratch = [
        pltpu.VMEM(chan_factor.shape, jnp.float32),
        pltpu.VMEM(cell_factor.shape, jnp.float32),
        pltpu.SemaphoreType.DMA((n_rel,)),
        pltpu.SemaphoreType.DMA((2,)),
    ]

    send, keep, rhs, slab_a = pl.pallas_call(
        functools.partial(pass_one_a, n_rel),
        in_specs=[hbm] * 3,
        out_specs=[WHOLE] * 4,
        out_shape=[half, half, tile, slab_half],
        scratch_shapes=scratch,
        compiler_params=PARAMS,
        cost_estimate=cost(4.5),
        name="pass_one_a",
    )(*inputs)
    chip_a = keep + trade(send, 1, n_chan)
    send, keep, stats, slab_b = pl.pallas_call(
        functools.partial(pass_one_b, start, all_rows, all_cols, n_cell, n_chan),
        in_specs=[hbm] * 3 + [WHOLE, pl.BlockSpec(memory_space=pl.ANY)],
        out_specs=[WHOLE] * 4,
        out_shape=[half, half, tile, slab_half],
        scratch_shapes=scratch,
        compiler_params=PARAMS,
        cost_estimate=cost(6),
        name="pass_one_b",
    )(*inputs, rhs, chip_a)
    chip_b = keep + trade(send, 1, n_chan)
    slabs = [pltpu.with_memory_space_constraint(x, pltpu.VMEM) for x in (slab_a, slab_b)]
    blocks_a, blocks_b = over_chan(chip_a, n_chan), over_chan(chip_b, n_chan)

    stats = pair_sum(over_cell(stats, n_cell))
    mask = 1
    while mask < n_chan:
        stats = stats + trade(stats, mask, n_chan)
        mask *= 2
    row, new_cell_gram, solved = pl.pallas_call(
        solve_one,
        in_specs=[WHOLE] * 2,
        out_specs=[WHOLE] * 3,
        out_shape=[f32((1, rank)), f32((rank, rank)), tile],
        compiler_params=SMALL,
        cost_estimate=cost(5.8),
        name="solve_one",
    )(stats, cell_gram_acc)

    late = [rel for rel in blocks_b if rel & 2]
    calls = [
        [((0, rel), x) for rel, x in blocks_a.items()] + [((1, rel), x) for rel, x in blocks_b.items() if rel not in late],
        [((1, rel), blocks_b[rel]) for rel in late],
    ]
    state = []
    for blocks in calls:
        where, pieces = zip(*blocks)
        n_in = 2 + CHUNKS + len(where)
        state = pl.pallas_call(
            functools.partial(pass_two, all_rows, all_cols, where, n_rel, bool(state)),
            in_specs=[WHOLE] * n_in + ([hbm, hbm, WHOLE] if state else []),
            out_specs=[hbm, hbm, WHOLE],
            out_shape=[f32((rank, rows)), f32((rank, rows)), f32((rank, cols + LANES))],
            scratch_shapes=[pltpu.VMEM((len(where), rank, width), jnp.float32)] * 2
            + [pltpu.SemaphoreType.DMA((2 * len(where),))],
            input_output_aliases={n_in: 0, n_in + 1: 1} if state else {},
            compiler_params=PARAMS,
            cost_estimate=cost(0.6 * len(where)),
            name="pass_two_b" if state else "pass_two_a",
        )(solved, cell_mttkrp, *slabs, *pieces, *state)
    new_cell_mttkrp, new_cell_factor, part = state

    parts = over_cell(part, n_cell)
    new_chan_mttkrp, new_chan_factor, new_chan_gram = pl.pallas_call(
        functools.partial(solve_two, all_rows, len(parts)),
        in_specs=[WHOLE] * (3 + len(parts)),
        out_specs=[WHOLE] * 3,
        out_shape=[f32((rank, cols)), f32((rank, cols)), f32((rank, rank))],
        compiler_params=SMALL,
        cost_estimate=cost(3.7),
        name="solve_two",
    )(solved, chan_mttkrp, chan_gram_acc, *parts)
    return (
        row.reshape(rank),
        new_cell_factor,
        new_chan_factor,
        new_cell_mttkrp,
        new_chan_mttkrp,
        new_cell_gram,
        new_chan_gram,
    )


def solution(mesh):
    placed = (
        P("cell", "chan"),
        P(None, "cell"),
        P(None, "chan"),
        P(None, "cell"),
        P(None, "chan"),
        P(),
        P(),
    )
    return jax.shard_map(
        body,
        mesh=mesh,
        in_specs=placed,
        out_specs=(
            P(),
            P(None, "cell"),
            P(None, "chan"),
            P(None, "cell"),
            P(None, "chan"),
            P(),
            P(),
        ),
        check_vma=False,
    )
```

time: 73.6 us -> 67.5 us (0.917)
  waiting for transfers between devices: 29.2 us -> 20.8 us
  Pallas kernels: 24.4 us -> 27.1 us
    ppermute x12 -> x15, waiting for transfers between devices: 18.6 us -> 13.9 us  [trade(): return lax.ppermute(x, 'chan', [(i, i ^ mask) for i in range(n_chan)])]
    ppermute x6, waiting for transfers between devices: 10.5 us -> 6.82 us  [over_cell(): lax.ppermute(x, 'cell', [(i, i ^ m) for i in range(n_cell)])]
    pallas_call x1 -> x2, Pallas kernels: 9.75 us -> 12.1 us  [the longest x1 7.15 us: body(): pl.pallas_call(functools.partial(pass_one_b, start, all_rows, all_cols, n...]
    ppermute x6, starting transfers between devices: 8.09 us -> 7.04 us  [over_cell(): lax.ppermute(x, 'cell', [(i, i ^ m) for i in range(n_cell)])]
    ppermute x12 -> x15, starting transfers between devices: 10.8 us -> 11.4 us  [trade(): return lax.ppermute(x, 'chan', [(i, i ^ mask) for i in range(n_chan)])]
    pallas_call x1 -> x2, Pallas kernels: 5.13 us -> 5.54 us  [body(): pl.pallas_call(functools.partial(pass_two, all_rows, all_cols, where, n_r...]
  transfers between devices with their start and end apart: 18 -> 21, of which waited for: 11 -> 9; matrix products, arithmetic and copies ran while one was open for 0% -> 0% of each run, Pallas kernels for 8% -> 25%
where the time goes in v3:
time: 67.5 us; the launch traced here: 67.4 us
  Pallas kernels  27.1 us (40%)
  waiting for transfers between devices  20.8 us (31%)
  starting transfers between devices  18.5 us (27%)
  between operations  0.83 us (1%)
    ppermute x15, waiting for transfers between devices, trade(): return lax.ppermute(x, 'chan', [(i, i ^ mask) for i in range(n_chan)])  13.9 us
    ppermute x15, starting transfers between devices, trade(): return lax.ppermute(x, 'chan', [(i, i ^ mask) for i in range(n_chan)])  11.4 us
    pallas_call x1, Pallas kernels, body(): pl.pallas_call(functools.partial(pass_one_b, start, all_rows, all_cols, n...  7.15 us
    ppermute x6, starting transfers between devices, over_cell(): lax.ppermute(x, 'cell', [(i, i ^ m) for i in range(n_cell)])  7.04 us
    ppermute x6, waiting for transfers between devices, over_cell(): lax.ppermute(x, 'cell', [(i, i ^ m) for i in range(n_cell)])  6.82 us
    pallas_call x1, Pallas kernels, body(): pl.pallas_call(solve_one, in_specs=[WHOLE] * 2, out_specs=[WHOLE] * 3, ou...  5.74 us
    pallas_call x2, Pallas kernels, body(): pl.pallas_call(functools.partial(pass_two, all_rows, all_cols, where, n_r...  5.54 us
    pallas_call x1, Pallas kernels, body(): pl.pallas_call(functools.partial(pass_one_a, n_rel), in_specs=[hbm] * 3,...  4.95 us
  transfers between devices with their start and end apart: 21, of which 9 were waited for; matrix products, arithmetic and copies ran while one was open for 0% of the time, Pallas kernels for 25%

profile of v3, /device:TPU:0, one launch (start us, length us, event | category | flops | bytes accessed | tf_op | source)
XLA Modules:
  0.0 67.4 jit_solution(13091957933566846195)
XLA Ops:
  0.6 5.0 %pass_one_a.1 = (f32[32,2048]{1,0:T(8,128)S(1)}, f32[32,2048]{1,0:T(8,128)S(1)}, f32[32,128]{1,0:T(8,128)S(1)}, bf16[4096,1024]{1,0:T(8,128)(2,1)S(1)}) custom-call(f32[32,1024]{1,0:T(8,128)} %chan_hbm.3, f32[32,8192]{1,0:T(8,128)} %cell_hbm.3, bf16[8192,1024]{1,0:T(8,128)(2,1)} %slab_hbm.3), custom_call_target="tpu_custom_call" | custom-call | flops 4499999744 | bytes 13500000 | tf_op jit(solution)/shard_map/pass_one_a/pallas_call | solution.py:219
  5.6 0.5 collective-permute-start
  6.1 1.2 %collective-permute-done = f32[32,2048]{1,0:T(8,128)S(1)} collective-permute-done((f32[32,2048]{1,0:T(8,128)S(1)}, f32[32,2048]{1,0:T(8,128)S(1)}, u32[]{:S(2)}, u32[]{:S(2)}) %collective-permute-start) | collective-permute-done | bytes 262176 | tf_op jit(solution)/shard_map/ppermute | solution.py:178
  7.3 3.0 %collective-permute-start.12 = (f32[32,1024]{1,0:T(8,128)S(1)}, f32[32,1024]{1,0:T(8,128)S(1)}, u32[]{:S(2)}, u32[]{:S(2)}) collective-permute-start(f32[32,1024]{1,0:T(8,128)S(1)} %slice.19), channel_id=1, source_target_pairs={{0,2},{1,3},{2,0},{3,1},{4,6},{5,7},{6,4},{7,5},{8,10},{9,11},{10,... | collective-permute-start | bytes 393224 | tf_op jit(solution)/shard_map/ppermute | solution.py:178
  10.3 0.0 copy-start.2
  10.3 7.2 %pass_one_b.1 = (f32[32,2048]{1,0:T(8,128)S(1)}, f32[32,2048]{1,0:T(8,128)S(1)}, f32[32,128]{1,0:T(8,128)S(1)}, bf16[4096,1024]{1,0:T(8,128)(2,1)S(1)}) custom-call(f32[32,1024]{1,0:T(8,128)} %chan_hbm.3, f32[32,8192]{1,0:T(8,128)} %cell_hbm.3, bf16[8192,1024]{1,0:T(8,128)(2,1)} %slab_hbm.3, f32[32,128]{1,0:T(8,128)S(1)} %get-tuple-element.27.rhs_in_ref, ...), custom_call_target="tpu_custom_call" | custom-call | flops 6000000000 | bytes 18000000 | tf_op jit(solution)/shard_map/pass_one_b/pallas_call | solution.py:230
  17.5 0.1 collective-permute-start.7
  17.6 0.0 collective-permute-done.12
  17.6 2.7 %collective-permute-start.13 = (f32[32,1024]{1,0:T(8,128)S(1)}, f32[32,1024]{1,0:T(8,128)S(1)}, u32[]{:S(2)}, u32[]{:S(2)}) collective-permute-start(f32[32,1024]{1,0:T(8,128)S(1)} %slice_add_fusion), channel_id=1, source_target_pairs={{0,4},{1,5},{2,6},{3,7},{4,0},{5,1},{6,2},{7,3},{8,12},{9,13},{10,... | collective-permute-start | bytes 393224 | tf_op jit(solution)/shard_map/ppermute | solution.py:178
  20.3 0.0 collective-permute-done.7
  20.3 0.5 collective-permute-start.8
  20.8 2.4 %collective-permute-start.3 = (f32[32,128]{1,0:T(8,128)S(1)}, f32[32,128]{1,0:T(8,128)S(1)}, u32[]{:S(2)}, u32[]{:S(2)}) collective-permute-start(f32[32,128]{1,0:T(8,128)S(1)} %get-tuple-element.30), channel_id=1, source_target_pairs={{0,24},{8,16},{16,8},{24,0},{1,25},{9,17},{17,9},{25,1},{2,26},{10... | collective-permute-start | bytes 49160 | tf_op jit(solution)/shard_map/ppermute | solution.py:168
  23.3 0.5 collective-permute-start.2
  23.8 0.5 collective-permute-start.1
  24.3 2.9 %collective-permute-done.13 = f32[32,1024]{1,0:T(8,128)S(1)} collective-permute-done((f32[32,1024]{1,0:T(8,128)S(1)}, f32[32,1024]{1,0:T(8,128)S(1)}, u32[]{:S(2)}, u32[]{:S(2)}) %collective-permute-start.13) | collective-permute-done | bytes 131104 | tf_op jit(solution)/shard_map/ppermute | solution.py:178
  27.2 0.1 collective-permute-start.14
  27.3 1.4 %collective-permute-done.8 = f32[32,1024]{1,0:T(8,128)S(1)} collective-permute-done((f32[32,1024]{1,0:T(8,128)S(1)}, f32[32,1024]{1,0:T(8,128)S(1)}, u32[]{:S(2)}, u32[]{:S(2)}) %collective-permute-start.8) | collective-permute-done | bytes 131104 | tf_op jit(solution)/shard_map/ppermute | solution.py:178
  28.7 1.8 %collective-permute-start.9 = (f32[32,1024]{1,0:T(8,128)S(1)}, f32[32,1024]{1,0:T(8,128)S(1)}, u32[]{:S(2)}, u32[]{:S(2)}) collective-permute-start(f32[32,1024]{1,0:T(8,128)S(1)} %slice_add_fusion.1), channel_id=1, source_target_pairs={{0,4},{1,5},{2,6},{3,7},{4,0},{5,1},{6,2},{7,3},{8,12},{9,13},{10,... | collective-permute-start | bytes 393224 | tf_op jit(solution)/shard_map/ppermute | solution.py:178
  30.5 0.0 collective-permute-done.3
  30.5 0.0 collective-permute-done.2
  30.5 0.0 collective-permute-done.1
  30.5 0.1 collective-permute-start.4
  30.6 1.2 %collective-permute-done.4 = f32[32,128]{1,0:T(8,128)S(1)} collective-permute-done((f32[32,128]{1,0:T(8,128)S(1)}, f32[32,128]{1,0:T(8,128)S(1)}, u32[]{:S(2)}, u32[]{:S(2)}) %collective-permute-start.4) | collective-permute-done | bytes 16416 | tf_op jit(solution)/shard_map/ppermute | solution.py:178
  31.8 0.0 collective-permute-start.5
  31.8 3.8 %collective-permute-done.5 = f32[32,128]{1,0:T(8,128)S(1)} collective-permute-done((f32[32,128]{1,0:T(8,128)S(1)}, f32[32,128]{1,0:T(8,128)S(1)}, u32[]{:S(2)}, u32[]{:S(2)}) %collective-permute-start.5) | collective-permute-done | bytes 16416 | tf_op jit(solution)/shard_map/ppermute | solution.py:178
  35.6 1.3 %collective-permute-start.6 = (f32[32,128]{1,0:T(8,128)S(1)}, f32[32,128]{1,0:T(8,128)S(1)}, u32[]{:S(2)}, u32[]{:S(2)}) collective-permute-start(f32[32,128]{1,0:T(8,128)S(1)} %add.41), channel_id=1, source_target_pairs={{0,4},{1,5},{2,6},{3,7},{4,0},{5,1},{6,2},{7,3},{8,12},{9,13},{10,... | collective-permute-start | bytes 49160 | tf_op jit(solution)/shard_map/ppermute | solution.py:178
  37.0 3.5 %collective-permute-done.6 = f32[32,128]{1,0:T(8,128)S(1)} collective-permute-done((f32[32,128]{1,0:T(8,128)S(1)}, f32[32,128]{1,0:T(8,128)S(1)}, u32[]{:S(2)}, u32[]{:S(2)}) %collective-permute-start.6) | collective-permute-done | bytes 16416 | tf_op jit(solution)/shard_map/ppermute | solution.py:178
  40.5 0.0 collective-permute-start.15
  40.5 0.0 collective-permute-done.14.refs_3_
  40.5 0.5 collective-permute-start.16
  41.0 0.0 collective-permute-done.9
  41.0 0.0 copy-start
  41.0 0.1 collective-permute-start.17
  41.1 0.5 collective-permute-start.10
  41.6 0.0 copy-done.2
  41.6 5.7 %solve_one.1 = (f32[1,32]{1,0:T(1,128)}, f32[32,32]{1,0:T(8,128)}, f32[32,128]{1,0:T(8,128)S(1)}) custom-call(f32[32,128]{1,0:T(8,128)S(1)} %add.42.stats_ref, f32[32,32]{1,0:T(8,128)S(1)} %copy-done.2), custom_call_target="tpu_custom_call" | custom-call | flops 5800000000 | bytes 17400000 | tf_op jit(solution)/shard_map/solve_one/pallas_call | solution.py:249
  47.4 0.0 collective-permute-done.10.refs_2_
  47.4 0.2 collective-permute-start.11
  47.6 0.0 collective-permute-done.15.refs_4_
  47.6 0.0 collective-permute-done.16.refs_5_
  47.6 0.0 collective-permute-done.17.refs_7_
  47.7 0.0 copy-done
  47.7 3.7 %pass_two_a.1 = (f32[32,8192]{1,0:T(8,128)}, f32[32,8192]{1,0:T(8,128)}, f32[32,1152]{1,0:T(8,128)S(1)}) custom-call(f32[32,128]{1,0:T(8,128)S(1)} %get-tuple-element.32.solved_ref, f32[32,8192]{1,0:T(8,128)S(1)} %copy-done, bf16[4096,1024]{1,0:T(8,128)(2,1)S(1)} %get-tuple-element.33.refs_0_, bf16[4096,1024]{1,0:T(8,128)(2,1)S(1)} %get-tuple-element.34.refs_1_, ...), custom_call_target="tpu_custom_call" | custom-call | flops 3600000000 | bytes 10799999 | tf_op jit(solution)/shard_map/pass_two_a/pallas_call | solution.py:268
  51.4 0.0 collective-permute-done.11.refs_3_
  51.4 0.0 copy-start.1
  51.4 0.0 copy-start.3
  51.5 1.8 %pass_two_b.1 = (f32[32,8192]{1,0:T(8,128)}, f32[32,8192]{1,0:T(8,128)}, f32[32,1152]{1,0:T(8,128)S(1)}) custom-call(f32[32,128]{1,0:T(8,128)S(1)} %get-tuple-element.32.solved_ref, f32[32,8192]{1,0:T(8,128)S(1)} %copy-done, bf16[4096,1024]{1,0:T(8,128)(2,1)S(1)} %get-tuple-element.33.refs_0_, ...), custom_call_target="tpu_custom_call", output_to_operand_aliasing={{0}: (6, {}), {1}: (7, {})} | custom-call | flops 1200000000 | bytes 3600000 | tf_op jit(solution)/shard_map/pass_two_b/pallas_call | solution.py:268
  53.3 2.6 %collective-permute-start.20 = (f32[32,1152]{1,0:T(8,128)S(1)}, f32[32,1152]{1,0:T(8,128)S(1)}, u32[]{:S(2)}, u32[]{:S(2)}) collective-permute-start(f32[32,1152]{1,0:T(8,128)S(1)} %get-tuple-element.41.refs_0_), channel_id=1, source_target_pairs={{0,24},{8,16},{16,8},{24,0},{1,25},{9,17},{17,9},{25,1},{2,26},{10... | collective-permute-start | bytes 442376 | tf_op jit(solution)/shard_map/ppermute | solution.py:168
  55.8 0.5 collective-permute-start.19
  56.3 0.5 collective-permute-start.18
  56.8 4.1 %collective-permute-done.20.refs_3_ = f32[32,1152]{1,0:T(8,128)S(1)} collective-permute-done((f32[32,1152]{1,0:T(8,128)S(1)}, f32[32,1152]{1,0:T(8,128)S(1)}, u32[]{:S(2)}, u32[]{:S(2)}) %collective-permute-start.20) | collective-permute-done | bytes 147488 | tf_op jit(solution)/shard_map/ppermute | solution.py:168
  60.9 2.6 %collective-permute-done.19.refs_2_ = f32[32,1152]{1,0:T(8,128)S(1)} collective-permute-done((f32[32,1152]{1,0:T(8,128)S(1)}, f32[32,1152]{1,0:T(8,128)S(1)}, u32[]{:S(2)}, u32[]{:S(2)}) %collective-permute-start.19) | collective-permute-done | bytes 147488 | tf_op jit(solution)/shard_map/ppermute | solution.py:168
  63.5 0.1 collective-permute-done.18.refs_1_
  63.6 0.0 copy-done.1
  63.6 0.0 copy-done.3
  63.6 3.7 %solve_two.1 = (f32[32,1024]{1,0:T(8,128)}, f32[32,1024]{1,0:T(8,128)}, f32[32,32]{1,0:T(8,128)}) custom-call(f32[32,128]{1,0:T(8,128)S(1)} %get-tuple-element.32.solved_ref, f32[32,1024]{1,0:T(8,128)S(1)} %copy-done.1, f32[32,32]{1,0:T(8,128)S(1)} %copy-done.3, f32[32,1152]{1,0:T(8,128)S(1)} %get-tuple-element.41.refs_0_, ...), custom_call_target="tpu_custom_call" | custom-call | flops 3700000000 | bytes 11100000 | tf_op jit(solution)/shard_map/solve_two/pallas_call | solution.py:283
  (12 shorter events, 0.2 us)
Async XLA Ops:
  5.6 1.7 %collective-permute-start = (f32[32,2048]{1,0:T(8,128)S(1)}, f32[32,2048]{1,0:T(8,128)S(1)}, u32[]{:S(2)}, u32[]{:S(2)}) collective-permute-start(f32[32,2048]{1,0:T(8,128)S(1)} %get-tuple-element.29), channel_id=1, source_target_pairs={{0,1},{1,0},{2,3},{3,2},{4,5},{5,4},{6,7},{7,6},{8,9},{9,8},{10,11... | collective-permute-start | bytes 786440 | tf_op jit(solution)/shard_map/ppermute | solution.py:178
  7.3 10.3 %collective-permute-start.12 = (f32[32,1024]{1,0:T(8,128)S(1)}, f32[32,1024]{1,0:T(8,128)S(1)}, u32[]{:S(2)}, u32[]{:S(2)}) collective-permute-start(f32[32,1024]{1,0:T(8,128)S(1)} %slice.19), channel_id=1, source_target_pairs={{0,2},{1,3},{2,0},{3,1},{4,6},{5,7},{6,4},{7,5},{8,10},{9,11},{10,... | collective-permute-start | bytes 393224 | tf_op jit(solution)/shard_map/ppermute | solution.py:178
  10.3 31.3 %copy-start.2 = (f32[32,32]{1,0:T(8,128)S(1)}, f32[32,32]{1,0:T(8,128)}, u32[]{:S(2)}) copy-start(f32[32,32]{1,0:T(8,128)} %acc_ref.2) | copy-start | bytes 12292
  17.5 2.8 %collective-permute-start.7 = (f32[32,2048]{1,0:T(8,128)S(1)}, f32[32,2048]{1,0:T(8,128)S(1)}, u32[]{:S(2)}, u32[]{:S(2)}) collective-permute-start(f32[32,2048]{1,0:T(8,128)S(1)} %get-tuple-element.36), channel_id=1, source_target_pairs={{0,1},{1,0},{2,3},{3,2},{4,5},{5,4},{6,7},{7,6},{8,9},{9,8},{10,11... | collective-permute-start | bytes 786440 | tf_op jit(solution)/shard_map/ppermute | solution.py:178
  17.6 9.6 %collective-permute-start.13 = (f32[32,1024]{1,0:T(8,128)S(1)}, f32[32,1024]{1,0:T(8,128)S(1)}, u32[]{:S(2)}, u32[]{:S(2)}) collective-permute-start(f32[32,1024]{1,0:T(8,128)S(1)} %slice_add_fusion), channel_id=1, source_target_pairs={{0,4},{1,5},{2,6},{3,7},{4,0},{5,1},{6,2},{7,3},{8,12},{9,13},{10,... | collective-permute-start | bytes 393224 | tf_op jit(solution)/shard_map/ppermute | solution.py:178
  20.3 8.4 %collective-permute-start.8 = (f32[32,1024]{1,0:T(8,128)S(1)}, f32[32,1024]{1,0:T(8,128)S(1)}, u32[]{:S(2)}, u32[]{:S(2)}) collective-permute-start(f32[32,1024]{1,0:T(8,128)S(1)} %slice.17), channel_id=1, source_target_pairs={{0,2},{1,3},{2,0},{3,1},{4,6},{5,7},{6,4},{7,5},{8,10},{9,11},{10,... | collective-permute-start | bytes 393224 | tf_op jit(solution)/shard_map/ppermute | solution.py:178
  20.8 9.7 %collective-permute-start.3 = (f32[32,128]{1,0:T(8,128)S(1)}, f32[32,128]{1,0:T(8,128)S(1)}, u32[]{:S(2)}, u32[]{:S(2)}) collective-permute-start(f32[32,128]{1,0:T(8,128)S(1)} %get-tuple-element.30), channel_id=1, source_target_pairs={{0,24},{8,16},{16,8},{24,0},{1,25},{9,17},{17,9},{25,1},{2,26},{10... | collective-permute-start | bytes 49160 | tf_op jit(solution)/shard_map/ppermute | solution.py:168
  23.3 7.2 %collective-permute-start.2 = (f32[32,128]{1,0:T(8,128)S(1)}, f32[32,128]{1,0:T(8,128)S(1)}, u32[]{:S(2)}, u32[]{:S(2)}) collective-permute-start(f32[32,128]{1,0:T(8,128)S(1)} %get-tuple-element.30), channel_id=1, source_target_pairs={{0,16},{8,24},{16,0},{24,8},{1,17},{9,25},{17,1},{25,9},{2,18},{10... | collective-permute-start | bytes 49160 | tf_op jit(solution)/shard_map/ppermute | solution.py:168
  23.8 6.7 %collective-permute-start.1 = (f32[32,128]{1,0:T(8,128)S(1)}, f32[32,128]{1,0:T(8,128)S(1)}, u32[]{:S(2)}, u32[]{:S(2)}) collective-permute-start(f32[32,128]{1,0:T(8,128)S(1)} %get-tuple-element.30), channel_id=1, source_target_pairs={{0,8},{8,0},{16,24},{24,16},{1,9},{9,1},{17,25},{25,17},{2,10},{10... | collective-permute-start | bytes 49160 | tf_op jit(solution)/shard_map/ppermute | solution.py:168
  27.2 13.2 %collective-permute-start.14 = (f32[32,1024]{1,0:T(8,128)S(1)}, f32[32,1024]{1,0:T(8,128)S(1)}, u32[]{:S(2)}, u32[]{:S(2)}) collective-permute-start(f32[32,1024]{1,0:T(8,128)S(1)} %add.47.refs_2_), channel_id=1, source_target_pairs={{0,2},{1,3},{2,0},{3,1},{4,6},{5,7},{6,4},{7,5},{8,10},{9,11},{10,... | collective-permute-start | bytes 393224 | tf_op jit(solution)/shard_map/ppermute | solution.py:178
  28.7 12.2 %collective-permute-start.9 = (f32[32,1024]{1,0:T(8,128)S(1)}, f32[32,1024]{1,0:T(8,128)S(1)}, u32[]{:S(2)}, u32[]{:S(2)}) collective-permute-start(f32[32,1024]{1,0:T(8,128)S(1)} %slice_add_fusion.1), channel_id=1, source_target_pairs={{0,4},{1,5},{2,6},{3,7},{4,0},{5,1},{6,2},{7,3},{8,12},{9,13},{10,... | collective-permute-start | bytes 393224 | tf_op jit(solution)/shard_map/ppermute | solution.py:178
  30.5 1.2 %collective-permute-start.4 = (f32[32,128]{1,0:T(8,128)S(1)}, f32[32,128]{1,0:T(8,128)S(1)}, u32[]{:S(2)}, u32[]{:S(2)}) collective-permute-start(f32[32,128]{1,0:T(8,128)S(1)} %add_add_fusion), channel_id=1, source_target_pairs={{0,1},{1,0},{2,3},{3,2},{4,5},{5,4},{6,7},{7,6},{8,9},{9,8},{10,11... | collective-permute-start | bytes 49160 | tf_op jit(solution)/shard_map/ppermute | solution.py:178
  31.8 3.9 %collective-permute-start.5 = (f32[32,128]{1,0:T(8,128)S(1)}, f32[32,128]{1,0:T(8,128)S(1)}, u32[]{:S(2)}, u32[]{:S(2)}) collective-permute-start(f32[32,128]{1,0:T(8,128)S(1)} %add.40), channel_id=1, source_target_pairs={{0,2},{1,3},{2,0},{3,1},{4,6},{5,7},{6,4},{7,5},{8,10},{9,11},{10,... | collective-permute-start | bytes 49160 | tf_op jit(solution)/shard_map/ppermute | solution.py:178
  35.6 4.8 %collective-permute-start.6 = (f32[32,128]{1,0:T(8,128)S(1)}, f32[32,128]{1,0:T(8,128)S(1)}, u32[]{:S(2)}, u32[]{:S(2)}) collective-permute-start(f32[32,128]{1,0:T(8,128)S(1)} %add.41), channel_id=1, source_target_pairs={{0,4},{1,5},{2,6},{3,7},{4,0},{5,1},{6,2},{7,3},{8,12},{9,13},{10,... | collective-permute-start | bytes 49160 | tf_op jit(solution)/shard_map/ppermute | solution.py:178
  40.5 7.2 %collective-permute-start.15 = (f32[32,1024]{1,0:T(8,128)S(1)}, f32[32,1024]{1,0:T(8,128)S(1)}, u32[]{:S(2)}, u32[]{:S(2)}) collective-permute-start(f32[32,1024]{1,0:T(8,128)S(1)} %add.47.refs_2_), channel_id=1, source_target_pairs={{0,1},{1,0},{2,3},{3,2},{4,5},{5,4},{6,7},{7,6},{8,9},{9,8},{10,11... | collective-permute-start | bytes 393224 | tf_op jit(solution)/shard_map/ppermute | solution.py:178
  40.5 7.2 %collective-permute-start.16 = (f32[32,1024]{1,0:T(8,128)S(1)}, f32[32,1024]{1,0:T(8,128)S(1)}, u32[]{:S(2)}, u32[]{:S(2)}) collective-permute-start(f32[32,1024]{1,0:T(8,128)S(1)} %collective-permute-done.14.refs_3_), channel_id=1, source_target_pairs={{0,1},{1,0},{2,3},{3,2},{4,5},{5,4},{6,7},{7,6},{8,9},{9,8},{10,11... | collective-permute-start | bytes 393224 | tf_op jit(solution)/shard_map/ppermute | solution.py:178
  41.0 6.7 %copy-start = (f32[32,8192]{1,0:T(8,128)S(1)}, f32[32,8192]{1,0:T(8,128)}, u32[]{:S(2)}) copy-start(f32[32,8192]{1,0:T(8,128)} %mttkrp_ref.4) | copy-start | bytes 3145732
  41.0 6.6 %collective-permute-start.17 = (f32[32,1024]{1,0:T(8,128)S(1)}, f32[32,1024]{1,0:T(8,128)S(1)}, u32[]{:S(2)}, u32[]{:S(2)}) collective-permute-start(f32[32,1024]{1,0:T(8,128)S(1)} %add.45.refs_6_), channel_id=1, source_target_pairs={{0,1},{1,0},{2,3},{3,2},{4,5},{5,4},{6,7},{7,6},{8,9},{9,8},{10,11... | collective-permute-start | bytes 393224 | tf_op jit(solution)/shard_map/ppermute | solution.py:178
  41.1 6.3 %collective-permute-start.10 = (f32[32,1024]{1,0:T(8,128)S(1)}, f32[32,1024]{1,0:T(8,128)S(1)}, u32[]{:S(2)}, u32[]{:S(2)}) collective-permute-start(f32[32,1024]{1,0:T(8,128)S(1)} %add.45.refs_6_), channel_id=1, source_target_pairs={{0,2},{1,3},{2,0},{3,1},{4,6},{5,7},{6,4},{7,5},{8,10},{9,11},{10,... | collective-permute-start | bytes 393224 | tf_op jit(solution)/shard_map/ppermute | solution.py:178
  47.4 4.0 %collective-permute-start.11 = (f32[32,1024]{1,0:T(8,128)S(1)}, f32[32,1024]{1,0:T(8,128)S(1)}, u32[]{:S(2)}, u32[]{:S(2)}) collective-permute-start(f32[32,1024]{1,0:T(8,128)S(1)} %collective-permute-done.10.refs_2_), channel_id=1, source_target_pairs={{0,1},{1,0},{2,3},{3,2},{4,5},{5,4},{6,7},{7,6},{8,9},{9,8},{10,11... | collective-permute-start | bytes 393224 | tf_op jit(solution)/shard_map/ppermute | solution.py:178
  51.4 12.2 %copy-start.1 = (f32[32,1024]{1,0:T(8,128)S(1)}, f32[32,1024]{1,0:T(8,128)}, u32[]{:S(2)}) copy-start(f32[32,1024]{1,0:T(8,128)} %mttkrp_ref.5) | copy-start | bytes 393220
  51.4 12.2 %copy-start.3 = (f32[32,32]{1,0:T(8,128)S(1)}, f32[32,32]{1,0:T(8,128)}, u32[]{:S(2)}) copy-start(f32[32,32]{1,0:T(8,128)} %acc_ref.3) | copy-start | bytes 12292
  53.3 7.6 %collective-permute-start.20 = (f32[32,1152]{1,0:T(8,128)S(1)}, f32[32,1152]{1,0:T(8,128)S(1)}, u32[]{:S(2)}, u32[]{:S(2)}) collective-permute-start(f32[32,1152]{1,0:T(8,128)S(1)} %get-tuple-element.41.refs_0_), channel_id=1, source_target_pairs={{0,24},{8,16},{16,8},{24,0},{1,25},{9,17},{17,9},{25,1},{2,26},{10... | collective-permute-start | bytes 442376 | tf_op jit(solution)/shard_map/ppermute | solution.py:168
  55.8 7.7 %collective-permute-start.19 = (f32[32,1152]{1,0:T(8,128)S(1)}, f32[32,1152]{1,0:T(8,128)S(1)}, u32[]{:S(2)}, u32[]{:S(2)}) collective-permute-start(f32[32,1152]{1,0:T(8,128)S(1)} %get-tuple-element.41.refs_0_), channel_id=1, source_target_pairs={{0,16},{8,24},{16,0},{24,8},{1,17},{9,25},{17,1},{25,9},{2,18},{10... | collective-permute-start | bytes 442376 | tf_op jit(solution)/shard_map/ppermute | solution.py:168
  56.3 7.3 %collective-permute-start.18 = (f32[32,1152]{1,0:T(8,128)S(1)}, f32[32,1152]{1,0:T(8,128)S(1)}, u32[]{:S(2)}, u32[]{:S(2)}) collective-permute-start(f32[32,1152]{1,0:T(8,128)S(1)} %get-tuple-element.41.refs_0_), channel_id=1, source_target_pairs={{0,8},{8,0},{16,24},{24,16},{1,9},{9,1},{17,25},{25,17},{2,10},{10... | collective-permute-start | bytes 442376 | tf_op jit(solution)/shard_map/ppermute | solution.py:168

commit v4 on v3

--- a/solution.py
+++ b/solution.py
@@ -29,12 +29,31 @@
     return (i == j).astype(jnp.float32)
 
 
-def eliminate(aug, n):
-    rows = lax.broadcasted_iota(jnp.int32, aug.shape, 0)
+def eliminate(matrix, right):
+    n = matrix.shape[0]
+    rows = lax.broadcasted_iota(jnp.int32, (n, LANES), 0)
+    spread = [jnp.broadcast_to(matrix[:, k : k + 1], (n, LANES)) for k in range(n)]
+    right = jnp.concatenate([right, jnp.zeros((n, LANES - right.shape[1]), jnp.float32)], axis=1)
     for k in range(n):
-        row = aug[k : k + 1, :] * (1.0 / aug[k : k + 1, k : k + 1])
-        aug = jnp.where(rows == k, row, aug - aug[:, k : k + 1] * row)
-    return aug[:, n:]
+        column = spread[k]
+        scale = 1.0 / column[k : k + 1, :]
+        at_k = rows == k
+
+        def clear(x):
+            row = x[k : k + 1, :] * scale
+            return jnp.where(at_k, row, x - column * row)
+
+        spread[k + 1 :] = [clear(x) for x in spread[k + 1 :]]
+        right = clear(right)
+    return right
+
+
+def gram(x):
+    high = x.astype(jnp.bfloat16)
+    low = (x - high.astype(jnp.float32)).astype(jnp.bfloat16)
+    dot = functools.partial(lax.dot_general, dimension_numbers=ROWS, preferred_element_type=jnp.float32)
+    cross = dot(high, low)
+    return dot(high, high) + (cross + cross.T)
 
 
 def place(rel, n_rel, width):
@@ -87,8 +106,8 @@
     load = copies([(chan_hbm, chan_ref), (cell_hbm, cell_ref)], small_sem)
     total = multiply(start, n_rel, chan_ref, cell_ref, slab_hbm, slab_v, sem, send_ref, keep_ref, load)
     chan, cell = chan_ref[...], cell_ref[...]
-    chan_gram = lax.dot_general(chan, chan, ROWS, precision=HI) / (all_cols * n_cell)
-    cell_gram = lax.dot_general(cell, cell, ROWS, precision=HI) / (all_rows * n_chan)
+    chan_gram = gram(chan) / (all_cols * n_cell)
+    cell_gram = gram(cell) / (all_rows * n_chan)
     total = total + rhs_in_ref[...]
     rhs = jnp.sum(total, axis=1, keepdims=True) / math.sqrt(all_rows * all_cols)
     pad = jnp.zeros((chan.shape[0], LANES - 1 - 2 * chan.shape[0]), jnp.float32)
@@ -99,11 +118,11 @@
     stats = stats_ref[...]
     n = stats.shape[0]
     cell_norm, chan_norm, rhs = stats[:, :n], stats[:, n : 2 * n], stats[:, 2 * n : 2 * n + 1]
-    time = eliminate(jnp.concatenate([cell_norm * chan_norm, rhs], axis=1), n)
+    time = eliminate(cell_norm * chan_norm, rhs)[:, :1]
     row = jnp.sum(eye(n) * time, axis=0, keepdims=True)
     outer = time * row
     gram = acc_ref[...] + chan_norm * outer
-    inverse = eliminate(jnp.concatenate([gram, eye(n)], axis=1), n)
+    inverse = eliminate(gram, eye(n))[:, :n]
     row_ref[...] = row
     gram_ref[...] = gram
     pad = jnp.zeros((n, LANES - 2 * n - 1), jnp.float32)
@@ -120,7 +139,7 @@
     inverse = solved_ref[:, :n]
     time = solved_ref[:, 2 * n : 2 * n + 1] / math.sqrt(all_cols)
     total = before[2][:, :cols] if resume else jnp.zeros((n, cols), jnp.float32)
-    gram = before[2][:, cols : cols + n] if resume else jnp.zeros((n, n), jnp.float32)
+    total_gram = before[2][:, cols : cols + n] if resume else jnp.zeros((n, n), jnp.float32)
     moves = []
     for i, ((chunk, rel), piece) in enumerate(zip(where, pieces)):
         width = piece.shape[1]
@@ -133,11 +152,11 @@
         for a, b in ((mttkrp_v, mttkrp_hbm), (factor_v, factor_hbm)):
             moves.append(pltpu.make_async_copy(a.at[i], b.at[:, rows], sem.at[len(moves)]))
             moves[-1].start()
-        gram += lax.dot_general(factor, factor, ROWS, precision=HI) / all_rows
+        total_gram += lax.dot_general(factor, factor, ROWS, precision=HI) / all_rows
         low = factor.astype(jnp.bfloat16)
         total += jnp.dot(low, slabs[chunk][pl.ds(at, width)], preferred_element_type=jnp.float32)
     out_ref[:, :cols] = total
-    out_ref[:, cols:] = jnp.concatenate([gram, jnp.zeros((n, LANES - n), jnp.float32)], axis=1)
+    out_ref[:, cols:] = jnp.concatenate([total_gram, jnp.zeros((n, LANES - n), jnp.float32)], axis=1)
     for move in moves:
         move.wait()
 
@@ -152,7 +171,7 @@
     outer = solved_ref[:, n : 2 * n]
     time = solved_ref[:, 2 * n : 2 * n + 1] / math.sqrt(all_rows)
     gram = acc_ref[...] + summed[:, cols : cols + n] * outer
-    inverse = eliminate(jnp.concatenate([gram, eye(n)], axis=1), n)
+    inverse = eliminate(gram, eye(n))[:, :n]
     right = mttkrp_ref[...] + time * summed[:, :cols]
     new_mttkrp[...] = right
     new_factor[...] = jnp.dot(inverse, right, precision=HI)
@@ -178,7 +197,11 @@
     return lax.ppermute(x, "chan", [(i, i ^ mask) for i in range(n_chan)])
 
 
-def over_chan(x, n_chan):
+def after(x, others):
+    return lax.optimization_barrier((x, others))[0]
+
+
+def halve(x, n_chan):
     width = x.shape[1] // (n_chan // 4)
     mask = 2
     while mask < n_chan // 2:
@@ -186,7 +209,12 @@
         keep, send = (jnp.concatenate(b, axis=1) if len(b) > 1 else b[0] for b in (blocks[::2], blocks[1::2]))
         x = keep + trade(send, mask, n_chan)
         mask *= 2
-    have = {0: x + trade(x, mask, n_chan)}
+    return x
+
+
+def give_back(x, n_chan):
+    have = {0: x}
+    mask = n_chan // 2
     while mask > 2:
         mask //= 2
         have.update({rel + mask: trade(block, mask, n_chan) for rel, block in list(have.items())})
@@ -234,18 +262,22 @@
         out_shape=[half, half, tile, slab_half],
         scratch_shapes=scratch,
         compiler_params=PARAMS,
-        cost_estimate=cost(6),
+        cost_estimate=cost(12),
         name="pass_one_b",
     )(*inputs, rhs, chip_a)
     chip_b = keep + trade(send, 1, n_chan)
     slabs = [pltpu.with_memory_space_constraint(x, pltpu.VMEM) for x in (slab_a, slab_b)]
-    blocks_a, blocks_b = over_chan(chip_a, n_chan), over_chan(chip_b, n_chan)
-
+    ready_a, ready_b = halve(chip_a, n_chan), halve(chip_b, n_chan)
+    last = n_chan // 2
+    stats = after(stats, (ready_a, chip_b))
     stats = pair_sum(over_cell(stats, n_cell))
+    total_a = ready_a + trade(ready_a, last, n_chan)
     mask = 1
     while mask < n_chan:
         stats = stats + trade(stats, mask, n_chan)
         mask *= 2
+    total_b = ready_b + trade(ready_b, last, n_chan)
+    blocks_a, blocks_b = give_back(total_a, n_chan), give_back(total_b, n_chan)
     row, new_cell_gram, solved = pl.pallas_call(
         solve_one,
         in_specs=[WHOLE] * 2,

time: 67.5 us -> 63 us (0.933)
  Pallas kernels: 27.1 us -> 20.4 us
  waiting for transfers between devices: 20.8 us -> 23.2 us
    pallas_call x1, Pallas kernels: 5.74 us -> 2.65 us  [body(): pl.pallas_call(solve_one, in_specs=[WHOLE] * 2, out_specs=[WHOLE] * 3, ou...]
    ppermute x15, waiting for transfers between devices: 13.9 us -> 16.3 us  [trade(): return lax.ppermute(x, 'chan', [(i, i ^ mask) for i in range(n_chan)])]
    pallas_call x1, Pallas kernels: 7.15 us -> 5.35 us  [body(): pl.pallas_call(functools.partial(pass_one_b, start, all_rows, all_cols, n...]
    pallas_call x1, Pallas kernels: 3.73 us -> 1.93 us  [body(): pl.pallas_call(functools.partial(solve_two, all_rows, len(parts)), in_spe...]
  transfers between devices with their start and end apart: 21 -> 21, of which waited for: 9 -> 10; matrix products, arithmetic and copies ran while one was open for 0% -> 0% of each run, Pallas kernels for 25% -> 19%
where the time goes in v4:
time: 63 us; the launch traced here: 62.9 us
  waiting for transfers between devices  23.2 us (37%)
  Pallas kernels  20.4 us (32%)
  starting transfers between devices  18.2 us (29%)
  between operations  0.84 us (1%)
    ppermute x15, waiting for transfers between devices, trade(): return lax.ppermute(x, 'chan', [(i, i ^ mask) for i in range(n_chan)])  16.3 us
    ppermute x15, starting transfers between devices, trade(): return lax.ppermute(x, 'chan', [(i, i ^ mask) for i in range(n_chan)])  11.2 us
    ppermute x6, starting transfers between devices, over_cell(): lax.ppermute(x, 'cell', [(i, i ^ m) for i in range(n_cell)])  7.04 us
    ppermute x6, waiting for transfers between devices, over_cell(): lax.ppermute(x, 'cell', [(i, i ^ m) for i in range(n_cell)])  6.93 us
    pallas_call x2, Pallas kernels, body(): pl.pallas_call(functools.partial(pass_two, all_rows, all_cols, where, n_r...  5.54 us
    pallas_call x1, Pallas kernels, body(): pl.pallas_call(functools.partial(pass_one_b, start, all_rows, all_cols, n...  5.35 us
    pallas_call x1, Pallas kernels, body(): pl.pallas_call(functools.partial(pass_one_a, n_rel), in_specs=[hbm] * 3,...  4.95 us
    pallas_call x1, Pallas kernels, body(): pl.pallas_call(solve_one, in_specs=[WHOLE] * 2, out_specs=[WHOLE] * 3, ou...  2.65 us
  transfers between devices with their start and end apart: 21, of which 10 were waited for; matrix products, arithmetic and copies ran while one was open for 0% of the time, Pallas kernels for 19%

profile of v4, /device:TPU:0, one launch (start us, length us, event | category | flops | bytes accessed | tf_op | source)
XLA Modules:
  0.0 62.9 jit_solution(917213819723920621)
XLA Ops:
  0.6 5.0 %pass_one_a.1 = (f32[32,2048]{1,0:T(8,128)S(1)}, f32[32,2048]{1,0:T(8,128)S(1)}, f32[32,128]{1,0:T(8,128)S(1)}, bf16[4096,1024]{1,0:T(8,128)(2,1)S(1)}) custom-call(f32[32,1024]{1,0:T(8,128)} %chan_hbm.3, f32[32,8192]{1,0:T(8,128)} %cell_hbm.3, bf16[8192,1024]{1,0:T(8,128)(2,1)} %slab_hbm.3), custom_call_target="tpu_custom_call" | custom-call | flops 4499999744 | bytes 13500000 | tf_op jit(solution)/shard_map/pass_one_a/pallas_call | solution.py:247
  5.6 0.5 collective-permute-start
  6.1 1.2 %collective-permute-done = f32[32,2048]{1,0:T(8,128)S(1)} collective-permute-done((f32[32,2048]{1,0:T(8,128)S(1)}, f32[32,2048]{1,0:T(8,128)S(1)}, u32[]{:S(2)}, u32[]{:S(2)}) %collective-permute-start) | collective-permute-done | bytes 262176 | tf_op jit(solution)/shard_map/ppermute | solution.py:197
  7.3 3.0 %collective-permute-start.1 = (f32[32,1024]{1,0:T(8,128)S(1)}, f32[32,1024]{1,0:T(8,128)S(1)}, u32[]{:S(2)}, u32[]{:S(2)}) collective-permute-start(f32[32,1024]{1,0:T(8,128)S(1)} %slice.17), channel_id=1, source_target_pairs={{0,2},{1,3},{2,0},{3,1},{4,6},{5,7},{6,4},{7,5},{8,10},{9,11},{10,... | collective-permute-start | bytes 393224 | tf_op jit(solution)/shard_map/ppermute | solution.py:197
  10.3 0.0 copy-start.2
  10.3 5.3 %pass_one_b.1 = (f32[32,2048]{1,0:T(8,128)S(1)}, f32[32,2048]{1,0:T(8,128)S(1)}, f32[32,128]{1,0:T(8,128)S(1)}, bf16[4096,1024]{1,0:T(8,128)(2,1)S(1)}) custom-call(f32[32,1024]{1,0:T(8,128)} %chan_hbm.3, f32[32,8192]{1,0:T(8,128)} %cell_hbm.3, bf16[8192,1024]{1,0:T(8,128)(2,1)} %slab_hbm.3, f32[32,128]{1,0:T(8,128)S(1)} %get-tuple-element.28.rhs_in_ref, ...), custom_call_target="tpu_custom_call" | custom-call | flops 12000000000 | bytes 36000000 | tf_op jit(solution)/shard_map/pass_one_b/pallas_call | solution.py:258
  15.7 0.1 collective-permute-start.2
  15.8 0.0 collective-permute-done.1
  15.8 2.7 %collective-permute-start.13 = (f32[32,1024]{1,0:T(8,128)S(1)}, f32[32,1024]{1,0:T(8,128)S(1)}, u32[]{:S(2)}, u32[]{:S(2)}) collective-permute-start(f32[32,1024]{1,0:T(8,128)S(1)} %slice_add_fusion.1), channel_id=1, source_target_pairs={{0,4},{1,5},{2,6},{3,7},{4,0},{5,1},{6,2},{7,3},{8,12},{9,13},{10,... | collective-permute-start | bytes 393224 | tf_op jit(solution)/shard_map/ppermute | solution.py:197
  18.5 0.0 collective-permute-done.2
  18.5 0.5 collective-permute-start.9
  19.0 2.4 %collective-permute-start.5 = (f32[32,128]{1,0:T(8,128)S(1)}, f32[32,128]{1,0:T(8,128)S(1)}, u32[]{:S(2)}, u32[]{:S(2)}) collective-permute-start(f32[32,128]{1,0:T(8,128)S(1)} %get-tuple-element.34), channel_id=1, source_target_pairs={{0,24},{8,16},{16,8},{24,0},{1,25},{9,17},{17,9},{25,1},{2,26},{10... | collective-permute-start | bytes 49160 | tf_op jit(solution)/shard_map/ppermute | solution.py:187
  21.5 0.5 collective-permute-start.4
  22.0 0.5 collective-permute-start.3
  22.5 2.9 %collective-permute-done.13 = f32[32,1024]{1,0:T(8,128)S(1)} collective-permute-done((f32[32,1024]{1,0:T(8,128)S(1)}, f32[32,1024]{1,0:T(8,128)S(1)}, u32[]{:S(2)}, u32[]{:S(2)}) %collective-permute-start.13) | collective-permute-done | bytes 131104 | tf_op jit(solution)/shard_map/ppermute | solution.py:197
  25.4 0.1 collective-permute-start.14
  25.5 1.4 %collective-permute-done.9 = f32[32,1024]{1,0:T(8,128)S(1)} collective-permute-done((f32[32,1024]{1,0:T(8,128)S(1)}, f32[32,1024]{1,0:T(8,128)S(1)}, u32[]{:S(2)}, u32[]{:S(2)}) %collective-permute-start.9) | collective-permute-done | bytes 131104 | tf_op jit(solution)/shard_map/ppermute | solution.py:197
  26.9 1.8 %collective-permute-start.10 = (f32[32,1024]{1,0:T(8,128)S(1)}, f32[32,1024]{1,0:T(8,128)S(1)}, u32[]{:S(2)}, u32[]{:S(2)}) collective-permute-start(f32[32,1024]{1,0:T(8,128)S(1)} %slice_add_fusion), channel_id=1, source_target_pairs={{0,4},{1,5},{2,6},{3,7},{4,0},{5,1},{6,2},{7,3},{8,12},{9,13},{10,... | collective-permute-start | bytes 393224 | tf_op jit(solution)/shard_map/ppermute | solution.py:197
  28.7 0.0 collective-permute-done.5
  28.7 0.0 collective-permute-done.4
  28.7 0.0 collective-permute-done.3
  28.7 0.1 collective-permute-start.6
  28.8 1.2 %collective-permute-done.6 = f32[32,128]{1,0:T(8,128)S(1)} collective-permute-done((f32[32,128]{1,0:T(8,128)S(1)}, f32[32,128]{1,0:T(8,128)S(1)}, u32[]{:S(2)}, u32[]{:S(2)}) %collective-permute-start.6) | collective-permute-done | bytes 16416 | tf_op jit(solution)/shard_map/ppermute | solution.py:197
  30.0 0.0 collective-permute-start.7
  30.0 3.8 %collective-permute-done.7 = f32[32,128]{1,0:T(8,128)S(1)} collective-permute-done((f32[32,128]{1,0:T(8,128)S(1)}, f32[32,128]{1,0:T(8,128)S(1)}, u32[]{:S(2)}, u32[]{:S(2)}) %collective-permute-start.7) | collective-permute-done | bytes 16416 | tf_op jit(solution)/shard_map/ppermute | solution.py:197
  33.8 1.3 %collective-permute-start.8 = (f32[32,128]{1,0:T(8,128)S(1)}, f32[32,128]{1,0:T(8,128)S(1)}, u32[]{:S(2)}, u32[]{:S(2)}) collective-permute-start(f32[32,128]{1,0:T(8,128)S(1)} %add.43), channel_id=1, source_target_pairs={{0,4},{1,5},{2,6},{3,7},{4,0},{5,1},{6,2},{7,3},{8,12},{9,13},{10,... | collective-permute-start | bytes 49160 | tf_op jit(solution)/shard_map/ppermute | solution.py:197
  35.2 0.0 collective-permute-start.15
  35.2 3.5 %collective-permute-done.8 = f32[32,128]{1,0:T(8,128)S(1)} collective-permute-done((f32[32,128]{1,0:T(8,128)S(1)}, f32[32,128]{1,0:T(8,128)S(1)}, u32[]{:S(2)}, u32[]{:S(2)}) %collective-permute-start.8) | collective-permute-done | bytes 16416 | tf_op jit(solution)/shard_map/ppermute | solution.py:197
  38.7 0.0 collective-permute-done.14.refs_3_
  38.7 0.1 collective-permute-start.16
  38.7 0.0 collective-permute-done.10
  38.8 0.0 copy-start
  38.8 0.5 collective-permute-start.17
  39.3 0.5 collective-permute-start.11
  39.8 0.0 copy-done.2
  39.8 2.6 %solve_one.1 = (f32[1,32]{1,0:T(1,128)}, f32[32,32]{1,0:T(8,128)}, f32[32,128]{1,0:T(8,128)S(1)}) custom-call(f32[32,128]{1,0:T(8,128)S(1)} %add.44.stats_ref, f32[32,32]{1,0:T(8,128)S(1)} %copy-done.2), custom_call_target="tpu_custom_call" | custom-call | flops 5800000000 | bytes 17400000 | tf_op jit(solution)/shard_map/solve_one/pallas_call | solution.py:281
  42.5 2.3 %collective-permute-done.11.refs_2_ = f32[32,1024]{1,0:T(8,128)S(1)} collective-permute-done((f32[32,1024]{1,0:T(8,128)S(1)}, f32[32,1024]{1,0:T(8,128)S(1)}, u32[]{:S(2)}, u32[]{:S(2)}) %collective-permute-start.11) | collective-permute-done | bytes 131104 | tf_op jit(solution)/shard_map/ppermute | solution.py:197
  44.8 0.0 collective-permute-start.12
  44.8 0.0 collective-permute-done.15.refs_4_
  44.8 0.0 collective-permute-done.16.refs_5_
  44.8 0.0 collective-permute-done.17.refs_7_
  44.8 0.0 copy-done
  44.8 3.7 %pass_two_a.1 = (f32[32,8192]{1,0:T(8,128)}, f32[32,8192]{1,0:T(8,128)}, f32[32,1152]{1,0:T(8,128)S(1)}) custom-call(f32[32,128]{1,0:T(8,128)S(1)} %get-tuple-element.36.solved_ref, f32[32,8192]{1,0:T(8,128)S(1)} %copy-done, bf16[4096,1024]{1,0:T(8,128)(2,1)S(1)} %get-tuple-element.37.refs_0_, bf16[4096,1024]{1,0:T(8,128)(2,1)S(1)} %get-tuple-element.38.refs_1_, ...), custom_call_target="tpu_custom_call" | custom-call | flops 3600000000 | bytes 10799999 | tf_op jit(solution)/shard_map/pass_two_a/pallas_call | solution.py:300
  48.6 0.0 collective-permute-done.12.refs_3_
  48.6 0.0 copy-start.1
  48.6 0.0 copy-start.3
  48.6 1.8 %pass_two_b.1 = (f32[32,8192]{1,0:T(8,128)}, f32[32,8192]{1,0:T(8,128)}, f32[32,1152]{1,0:T(8,128)S(1)}) custom-call(f32[32,128]{1,0:T(8,128)S(1)} %get-tuple-element.36.solved_ref, f32[32,8192]{1,0:T(8,128)S(1)} %copy-done, bf16[4096,1024]{1,0:T(8,128)(2,1)S(1)} %get-tuple-element.37.refs_0_, ...), custom_call_target="tpu_custom_call", output_to_operand_aliasing={{0}: (6, {}), {1}: (7, {})} | custom-call | flops 1200000000 | bytes 3600000 | tf_op jit(solution)/shard_map/pass_two_b/pallas_call | solution.py:300
  50.4 2.5 %collective-permute-start.20 = (f32[32,1152]{1,0:T(8,128)S(1)}, f32[32,1152]{1,0:T(8,128)S(1)}, u32[]{:S(2)}, u32[]{:S(2)}) collective-permute-start(f32[32,1152]{1,0:T(8,128)S(1)} %get-tuple-element.43.refs_0_), channel_id=1, source_target_pairs={{0,24},{8,16},{16,8},{24,0},{1,25},{9,17},{17,9},{25,1},{2,26},{10... | collective-permute-start | bytes 442376 | tf_op jit(solution)/shard_map/ppermute | solution.py:187
  53.0 0.5 collective-permute-start.19
  53.5 0.5 collective-permute-start.18
  54.0 4.1 %collective-permute-done.20.refs_3_ = f32[32,1152]{1,0:T(8,128)S(1)} collective-permute-done((f32[32,1152]{1,0:T(8,128)S(1)}, f32[32,1152]{1,0:T(8,128)S(1)}, u32[]{:S(2)}, u32[]{:S(2)}) %collective-permute-start.20) | collective-permute-done | bytes 147488 | tf_op jit(solution)/shard_map/ppermute | solution.py:187
  58.1 2.8 %collective-permute-done.19.refs_2_ = f32[32,1152]{1,0:T(8,128)S(1)} collective-permute-done((f32[32,1152]{1,0:T(8,128)S(1)}, f32[32,1152]{1,0:T(8,128)S(1)}, u32[]{:S(2)}, u32[]{:S(2)}) %collective-permute-start.19) | collective-permute-done | bytes 147488 | tf_op jit(solution)/shard_map/ppermute | solution.py:187
  60.8 0.1 collective-permute-done.18.refs_1_
  60.9 0.0 copy-done.1
  60.9 0.0 copy-done.3
  60.9 1.9 %solve_two.1 = (f32[32,1024]{1,0:T(8,128)}, f32[32,1024]{1,0:T(8,128)}, f32[32,32]{1,0:T(8,128)}) custom-call(f32[32,128]{1,0:T(8,128)S(1)} %get-tuple-element.36.solved_ref, f32[32,1024]{1,0:T(8,128)S(1)} %copy-done.1, f32[32,32]{1,0:T(8,128)S(1)} %copy-done.3, f32[32,1152]{1,0:T(8,128)S(1)} %get-tuple-element.43.refs_0_, ...), custom_call_target="tpu_custom_call" | custom-call | flops 3700000000 | bytes 11100000 | tf_op jit(solution)/shard_map/solve_two/pallas_call | solution.py:315
  (12 shorter events, 0.2 us)
Async XLA Ops:
  5.6 1.7 %collective-permute-start = (f32[32,2048]{1,0:T(8,128)S(1)}, f32[32,2048]{1,0:T(8,128)S(1)}, u32[]{:S(2)}, u32[]{:S(2)}) collective-permute-start(f32[32,2048]{1,0:T(8,128)S(1)} %get-tuple-element.30), channel_id=1, source_target_pairs={{0,1},{1,0},{2,3},{3,2},{4,5},{5,4},{6,7},{7,6},{8,9},{9,8},{10,11... | collective-permute-start | bytes 786440 | tf_op jit(solution)/shard_map/ppermute | solution.py:197
  7.3 8.5 %collective-permute-start.1 = (f32[32,1024]{1,0:T(8,128)S(1)}, f32[32,1024]{1,0:T(8,128)S(1)}, u32[]{:S(2)}, u32[]{:S(2)}) collective-permute-start(f32[32,1024]{1,0:T(8,128)S(1)} %slice.17), channel_id=1, source_target_pairs={{0,2},{1,3},{2,0},{3,1},{4,6},{5,7},{6,4},{7,5},{8,10},{9,11},{10,... | collective-permute-start | bytes 393224 | tf_op jit(solution)/shard_map/ppermute | solution.py:197
  10.3 29.5 %copy-start.2 = (f32[32,32]{1,0:T(8,128)S(1)}, f32[32,32]{1,0:T(8,128)}, u32[]{:S(2)}) copy-start(f32[32,32]{1,0:T(8,128)} %acc_ref.2) | copy-start | bytes 12292
  15.7 2.8 %collective-permute-start.2 = (f32[32,2048]{1,0:T(8,128)S(1)}, f32[32,2048]{1,0:T(8,128)S(1)}, u32[]{:S(2)}, u32[]{:S(2)}) collective-permute-start(f32[32,2048]{1,0:T(8,128)S(1)} %get-tuple-element.33), channel_id=1, source_target_pairs={{0,1},{1,0},{2,3},{3,2},{4,5},{5,4},{6,7},{7,6},{8,9},{9,8},{10,11... | collective-permute-start | bytes 786440 | tf_op jit(solution)/shard_map/ppermute | solution.py:197
  15.8 9.6 %collective-permute-start.13 = (f32[32,1024]{1,0:T(8,128)S(1)}, f32[32,1024]{1,0:T(8,128)S(1)}, u32[]{:S(2)}, u32[]{:S(2)}) collective-permute-start(f32[32,1024]{1,0:T(8,128)S(1)} %slice_add_fusion.1), channel_id=1, source_target_pairs={{0,4},{1,5},{2,6},{3,7},{4,0},{5,1},{6,2},{7,3},{8,12},{9,13},{10,... | collective-permute-start | bytes 393224 | tf_op jit(solution)/shard_map/ppermute | solution.py:197
  18.5 8.4 %collective-permute-start.9 = (f32[32,1024]{1,0:T(8,128)S(1)}, f32[32,1024]{1,0:T(8,128)S(1)}, u32[]{:S(2)}, u32[]{:S(2)}) collective-permute-start(f32[32,1024]{1,0:T(8,128)S(1)} %slice.19), channel_id=1, source_target_pairs={{0,2},{1,3},{2,0},{3,1},{4,6},{5,7},{6,4},{7,5},{8,10},{9,11},{10,... | collective-permute-start | bytes 393224 | tf_op jit(solution)/shard_map/ppermute | solution.py:197
  19.0 9.7 %collective-permute-start.5 = (f32[32,128]{1,0:T(8,128)S(1)}, f32[32,128]{1,0:T(8,128)S(1)}, u32[]{:S(2)}, u32[]{:S(2)}) collective-permute-start(f32[32,128]{1,0:T(8,128)S(1)} %get-tuple-element.34), channel_id=1, source_target_pairs={{0,24},{8,16},{16,8},{24,0},{1,25},{9,17},{17,9},{25,1},{2,26},{10... | collective-permute-start | bytes 49160 | tf_op jit(solution)/shard_map/ppermute | solution.py:187
  21.5 7.2 %collective-permute-start.4 = (f32[32,128]{1,0:T(8,128)S(1)}, f32[32,128]{1,0:T(8,128)S(1)}, u32[]{:S(2)}, u32[]{:S(2)}) collective-permute-start(f32[32,128]{1,0:T(8,128)S(1)} %get-tuple-element.34), channel_id=1, source_target_pairs={{0,16},{8,24},{16,0},{24,8},{1,17},{9,25},{17,1},{25,9},{2,18},{10... | collective-permute-start | bytes 49160 | tf_op jit(solution)/shard_map/ppermute | solution.py:187
  22.0 6.7 %collective-permute-start.3 = (f32[32,128]{1,0:T(8,128)S(1)}, f32[32,128]{1,0:T(8,128)S(1)}, u32[]{:S(2)}, u32[]{:S(2)}) collective-permute-start(f32[32,128]{1,0:T(8,128)S(1)} %get-tuple-element.34), channel_id=1, source_target_pairs={{0,8},{8,0},{16,24},{24,16},{1,9},{9,1},{17,25},{25,17},{2,10},{10... | collective-permute-start | bytes 49160 | tf_op jit(solution)/shard_map/ppermute | solution.py:187
  25.4 13.2 %collective-permute-start.14 = (f32[32,1024]{1,0:T(8,128)S(1)}, f32[32,1024]{1,0:T(8,128)S(1)}, u32[]{:S(2)}, u32[]{:S(2)}) collective-permute-start(f32[32,1024]{1,0:T(8,128)S(1)} %add.47.refs_2_), channel_id=1, source_target_pairs={{0,2},{1,3},{2,0},{3,1},{4,6},{5,7},{6,4},{7,5},{8,10},{9,11},{10,... | collective-permute-start | bytes 393224 | tf_op jit(solution)/shard_map/ppermute | solution.py:197
  26.9 11.8 %collective-permute-start.10 = (f32[32,1024]{1,0:T(8,128)S(1)}, f32[32,1024]{1,0:T(8,128)S(1)}, u32[]{:S(2)}, u32[]{:S(2)}) collective-permute-start(f32[32,1024]{1,0:T(8,128)S(1)} %slice_add_fusion), channel_id=1, source_target_pairs={{0,4},{1,5},{2,6},{3,7},{4,0},{5,1},{6,2},{7,3},{8,12},{9,13},{10,... | collective-permute-start | bytes 393224 | tf_op jit(solution)/shard_map/ppermute | solution.py:197
  28.7 1.2 %collective-permute-start.6 = (f32[32,128]{1,0:T(8,128)S(1)}, f32[32,128]{1,0:T(8,128)S(1)}, u32[]{:S(2)}, u32[]{:S(2)}) collective-permute-start(f32[32,128]{1,0:T(8,128)S(1)} %add_add_fusion), channel_id=1, source_target_pairs={{0,1},{1,0},{2,3},{3,2},{4,5},{5,4},{6,7},{7,6},{8,9},{9,8},{10,11... | collective-permute-start | bytes 49160 | tf_op jit(solution)/shard_map/ppermute | solution.py:197
  30.0 3.9 %collective-permute-start.7 = (f32[32,128]{1,0:T(8,128)S(1)}, f32[32,128]{1,0:T(8,128)S(1)}, u32[]{:S(2)}, u32[]{:S(2)}) collective-permute-start(f32[32,128]{1,0:T(8,128)S(1)} %add.42), channel_id=1, source_target_pairs={{0,2},{1,3},{2,0},{3,1},{4,6},{5,7},{6,4},{7,5},{8,10},{9,11},{10,... | collective-permute-start | bytes 49160 | tf_op jit(solution)/shard_map/ppermute | solution.py:197
  33.8 4.8 %collective-permute-start.8 = (f32[32,128]{1,0:T(8,128)S(1)}, f32[32,128]{1,0:T(8,128)S(1)}, u32[]{:S(2)}, u32[]{:S(2)}) collective-permute-start(f32[32,128]{1,0:T(8,128)S(1)} %add.43), channel_id=1, source_target_pairs={{0,4},{1,5},{2,6},{3,7},{4,0},{5,1},{6,2},{7,3},{8,12},{9,13},{10,... | collective-permute-start | bytes 49160 | tf_op jit(solution)/shard_map/ppermute | solution.py:197
  35.2 9.6 %collective-permute-start.15 = (f32[32,1024]{1,0:T(8,128)S(1)}, f32[32,1024]{1,0:T(8,128)S(1)}, u32[]{:S(2)}, u32[]{:S(2)}) collective-permute-start(f32[32,1024]{1,0:T(8,128)S(1)} %add.47.refs_2_), channel_id=1, source_target_pairs={{0,1},{1,0},{2,3},{3,2},{4,5},{5,4},{6,7},{7,6},{8,9},{9,8},{10,11... | collective-permute-start | bytes 393224 | tf_op jit(solution)/shard_map/ppermute | solution.py:197
  38.7 6.2 %collective-permute-start.16 = (f32[32,1024]{1,0:T(8,128)S(1)}, f32[32,1024]{1,0:T(8,128)S(1)}, u32[]{:S(2)}, u32[]{:S(2)}) collective-permute-start(f32[32,1024]{1,0:T(8,128)S(1)} %collective-permute-done.14.refs_3_), channel_id=1, source_target_pairs={{0,1},{1,0},{2,3},{3,2},{4,5},{5,4},{6,7},{7,6},{8,9},{9,8},{10,11... | collective-permute-start | bytes 393224 | tf_op jit(solution)/shard_map/ppermute | solution.py:197
  38.8 6.1 %copy-start = (f32[32,8192]{1,0:T(8,128)S(1)}, f32[32,8192]{1,0:T(8,128)}, u32[]{:S(2)}) copy-start(f32[32,8192]{1,0:T(8,128)} %mttkrp_ref.4) | copy-start | bytes 3145732
  38.8 6.0 %collective-permute-start.17 = (f32[32,1024]{1,0:T(8,128)S(1)}, f32[32,1024]{1,0:T(8,128)S(1)}, u32[]{:S(2)}, u32[]{:S(2)}) collective-permute-start(f32[32,1024]{1,0:T(8,128)S(1)} %add.46.refs_6_), channel_id=1, source_target_pairs={{0,1},{1,0},{2,3},{3,2},{4,5},{5,4},{6,7},{7,6},{8,9},{9,8},{10,11... | collective-permute-start | bytes 393224 | tf_op jit(solution)/shard_map/ppermute | solution.py:197
  39.3 5.5 %collective-permute-start.11 = (f32[32,1024]{1,0:T(8,128)S(1)}, f32[32,1024]{1,0:T(8,128)S(1)}, u32[]{:S(2)}, u32[]{:S(2)}) collective-permute-start(f32[32,1024]{1,0:T(8,128)S(1)} %add.46.refs_6_), channel_id=1, source_target_pairs={{0,2},{1,3},{2,0},{3,1},{4,6},{5,7},{6,4},{7,5},{8,10},{9,11},{10,... | collective-permute-start | bytes 393224 | tf_op jit(solution)/shard_map/ppermute | solution.py:197
  44.8 3.8 %collective-permute-start.12 = (f32[32,1024]{1,0:T(8,128)S(1)}, f32[32,1024]{1,0:T(8,128)S(1)}, u32[]{:S(2)}, u32[]{:S(2)}) collective-permute-start(f32[32,1024]{1,0:T(8,128)S(1)} %collective-permute-done.11.refs_2_), channel_id=1, source_target_pairs={{0,1},{1,0},{2,3},{3,2},{4,5},{5,4},{6,7},{7,6},{8,9},{9,8},{10,11... | collective-permute-start | bytes 393224 | tf_op jit(solution)/shard_map/ppermute | solution.py:197
  48.6 12.3 %copy-start.1 = (f32[32,1024]{1,0:T(8,128)S(1)}, f32[32,1024]{1,0:T(8,128)}, u32[]{:S(2)}) copy-start(f32[32,1024]{1,0:T(8,128)} %mttkrp_ref.5) | copy-start | bytes 393220
  48.6 12.3 %copy-start.3 = (f32[32,32]{1,0:T(8,128)S(1)}, f32[32,32]{1,0:T(8,128)}, u32[]{:S(2)}) copy-start(f32[32,32]{1,0:T(8,128)} %acc_ref.3) | copy-start | bytes 12292
  50.4 7.6 %collective-permute-start.20 = (f32[32,1152]{1,0:T(8,128)S(1)}, f32[32,1152]{1,0:T(8,128)S(1)}, u32[]{:S(2)}, u32[]{:S(2)}) collective-permute-start(f32[32,1152]{1,0:T(8,128)S(1)} %get-tuple-element.43.refs_0_), channel_id=1, source_target_pairs={{0,24},{8,16},{16,8},{24,0},{1,25},{9,17},{17,9},{25,1},{2,26},{10... | collective-permute-start | bytes 442376 | tf_op jit(solution)/shard_map/ppermute | solution.py:187
  53.0 7.9 %collective-permute-start.19 = (f32[32,1152]{1,0:T(8,128)S(1)}, f32[32,1152]{1,0:T(8,128)S(1)}, u32[]{:S(2)}, u32[]{:S(2)}) collective-permute-start(f32[32,1152]{1,0:T(8,128)S(1)} %get-tuple-element.43.refs_0_), channel_id=1, source_target_pairs={{0,16},{8,24},{16,0},{24,8},{1,17},{9,25},{17,1},{25,9},{2,18},{10... | collective-permute-start | bytes 442376 | tf_op jit(solution)/shard_map/ppermute | solution.py:187
  53.5 7.5 %collective-permute-start.18 = (f32[32,1152]{1,0:T(8,128)S(1)}, f32[32,1152]{1,0:T(8,128)S(1)}, u32[]{:S(2)}, u32[]{:S(2)}) collective-permute-start(f32[32,1152]{1,0:T(8,128)S(1)} %get-tuple-element.43.refs_0_), channel_id=1, source_target_pairs={{0,8},{8,0},{16,24},{24,16},{1,9},{9,1},{17,25},{25,17},{2,10},{10... | collective-permute-start | bytes 442376 | tf_op jit(solution)/shard_map/ppermute | solution.py:187
